TPU v7x, 128 devices: a whole 4x4x4 slice. The times are simulated.
128 devices in a mesh: depth: 8 (over z, x_hi), dp: 16 (over y, x_lo, core).
Axes of the slice: x: 4 (x_hi: 2, x_lo: 2; x = x_hi * 2 + x_lo), y: 4, z: 4, core: 2. Of those that a mesh axis runs over, the one named last changes fastest.
Arguments:
- layer_inputs: float32 [8, 6144, 2048], P('depth', 'dp'), may hold values from -6 to 6
- weights: float32 [8, 2048, 2048], P('depth', 'dp'), may hold values from -6 to 6
- offsets: float32 [8, 2048], P('depth', 'dp'), may hold values from -3 to 3
- layer_outputs: float32 [8, 6144, 2048], P('depth', 'dp'), may hold values from 0 to 2
- multipliers: float32 [8, 6144, 2048], P('depth', 'dp'), may hold values from -3 to 3
Outputs:
- new_inputs: float32 [8, 6144, 2048], P('depth', 'dp')
- new_weights: float32 [8, 2048, 2048], P('depth', 'dp')
- new_offsets: float32 [8, 2048], P('depth', 'dp')
- new_outputs: float32 [8, 6144, 2048], P('depth', 'dp')
- new_multipliers: float32 [8, 6144, 2048], P('depth', 'dp')
All inputs are finite; a program needn't handle non-finite values.
Results may differ from a plain program's by a relative error of at most 0.00008.
Values sent between devices are 32-bit elements; how exact they have to be, the bound alone decides.
No kernel may reach another device: no remote copies, remote signals or barrier semaphores. Data moves between devices by JAX's collectives and lax.ppermute only.
A program may use at most 128 MiB of HBM per device.

v0:
```python
import math

import jax
import jax.numpy as jnp
from jax import lax
from jax.sharding import PartitionSpec as P

D = 2048


fit_weight = 1.0
penalty = 1.0
step_input = 0.5


def passed_along(block, axis, distance):
    devices = range(lax.axis_size(axis))
    route = [(i - distance, i) for i in devices if i - distance in devices]
    return lax.ppermute(block, axis, route)


def side_by_side(arrays, axis, dim, along):
    widths = [math.prod(a.shape[along:]) for a in arrays]
    both = jnp.concatenate(
        [a.reshape(*a.shape[:along], w) for a, w in zip(arrays, widths)], axis=along
    )
    out = lax.all_gather(both, axis, axis=dim, tiled=True)
    tiles = jnp.split(out, [sum(widths[:k]) for k in range(1, len(widths))], axis=along)
    return tuple((b.reshape(*out.shape[:along], *a.shape[along:]) for a, b in zip(arrays, tiles)))


def in_one_piece(arrays, axis, dim, along):
    widths = [math.prod(a.shape[along:]) for a in arrays]
    both = jnp.concatenate(
        [a.reshape(*a.shape[:along], w) for a, w in zip(arrays, widths)], axis=along
    )
    out = lax.psum_scatter(both, axis, scatter_dimension=dim, tiled=True)
    tiles = jnp.split(out, [sum(widths[:k]) for k in range(1, len(widths))], axis=along)
    return tuple((b.reshape(*out.shape[:along], *a.shape[along:]) for a, b in zip(arrays, tiles)))


def body(layer_inputs, weights, offsets, layer_outputs, multipliers):
    highest = lax.Precision.HIGHEST
    scaling = 1.0 / math.sqrt(D)
    inputs_here = layer_inputs[0]
    outputs_here = layer_outputs[0]
    mults_here = multipliers[0]
    row_count = inputs_here.shape[0]
    samples = row_count * lax.axis_size("dp")
    step_weight = 8.0 / math.sqrt(samples)
    step_offset = 0.5 / math.sqrt(samples)
    prev_outputs, prev_mults = passed_along((layer_outputs, multipliers), "depth", 1)
    whole_weight, whole_offset = side_by_side((weights, offsets), "dp", 1, 2)
    affine = (
        scaling * jnp.dot(inputs_here, whole_weight[0].T, precision=highest)
        + whole_offset[0][None, :]
    )
    misfit = affine - outputs_here
    pulled = scaling * jnp.dot(misfit, whole_weight[0], precision=highest)
    layer_index = lax.axis_index("depth")
    is_first = layer_index == 0
    is_last = layer_index == lax.axis_size("depth") - 1
    pull_term = fit_weight * pulled
    gradient = pull_term + prev_mults[0] + penalty * (inputs_here - prev_outputs[0])
    stepped = inputs_here - step_input * gradient
    inputs_new = jnp.where(is_first, inputs_here, stepped)
    next_block = passed_along(inputs_new[None], "depth", -1)
    next_inputs = next_block[0]
    weight_grad = fit_weight * scaling * jnp.dot(misfit.T, inputs_here, precision=highest)
    offset_grad = fit_weight * jnp.sum(misfit, axis=0)
    weight_sum, offset_sum = in_one_piece((weight_grad, offset_grad), "dp", 0, 1)
    weights_new = weights - step_weight * weight_sum[None]
    offsets_new = offsets - step_offset * offset_sum[None]
    coupled = jnp.maximum(
        0.0, (fit_weight * affine + penalty * next_inputs + mults_here) / (fit_weight + penalty)
    )
    outputs_new = jnp.where(is_last, jnp.maximum(0.0, affine), coupled)
    mults_new = jnp.where(is_last, mults_here, mults_here + penalty * (next_inputs - outputs_new))
    return (inputs_new[None], weights_new, offsets_new, outputs_new[None], mults_new[None])


def solution(mesh):
    in_specs = (
        P("depth", "dp", None),
        P("depth", "dp", None),
        P("depth", "dp"),
        P("depth", "dp", None),
        P("depth", "dp", None),
    )
    out_specs = (
        P("depth", "dp", None),
        P("depth", "dp", None),
        P("depth", "dp"),
        P("depth", "dp", None),
        P("depth", "dp", None),
    )
    return jax.shard_map(body, mesh=mesh, in_specs=in_specs, out_specs=out_specs, check_vma=False)
```

profile of v0, /device:TPU:0, one launch (start us, length us, event | category | flops | bytes accessed | tf_op | source)
XLA Modules:
  0.0 545.6 jit_solution(1633590904640079947)
XLA Ops:
  7.2 0.0 all-gather.2.cloned.1.call-start
  7.2 0.9 copy.13
  8.1 2.3 pad_maximum_fusion.1
  10.4 0.0 all-gather.2.cloned.1.call-update
  10.5 0.0 reduce-scatter.2.cloned.1.call-start
  10.5 6.7 %collective-permute-start = (f32[1,384,2048]{2,1,0:T(8,128)}, f32[1,384,2048]{2,1,0:T(8,128)}, u32[]{:S(2)}, u32[]{:S(2)}) collective-permute-start(f32[1,384,2048]{2,1,0:T(8,128)} %param.9), channel_id=1, source_target_pairs={{0,16},{16,32},{32,48},{48,64},{64,80},{80,96},{96,112},{1,17},{17... | collective-permute-start | bytes 9437192 | tf_op jit(solution)/shard_map/ppermute | solution.py:19
  17.2 3.7 collective-permute-start.1
  20.9 172.2 %all-gather.2.cloned.1.call-done = f32[1,2048,2049]{2,1,0:T(8,128)} async-done(((f32[1,128,2049]{2,1,0:T(8,128)}), f32[1,2048,2049]{2,1,0:T(8,128)}) %all-gather.2.cloned.1.call-update) | async-done | bytes 16785424 | tf_op jit(solution)/shard_map/all_gather | solution.py:27
  193.1 1.6 slice_reduce_fusion
  194.7 24.1 %multiply_add_fusion = f32[2048,384]{0,1:T(8,128)S(1)} fusion(f32[1,384,2048]{2,1,0:T(8,128)} %param.5, f32[1,2048,2049]{2,1,0:T(8,128)} %all-gather.2.cloned.1.call-done, f32[2048]{0:T(1024)S(1)} %slice_reduce_fusion), kind=kOutput, calls=%fused_computation.23 | convolution fusion | flops 19328925696 | bytes 23076864 | tf_op jit(solution)/shard_map/dot_general | solution.py:55
  218.8 15.3 %collective-permute-done.1 = f32[1,384,2048]{2,1,0:T(8,128)} collective-permute-done((f32[1,384,2048]{2,1,0:T(8,128)S(1)}, f32[1,384,2048]{2,1,0:T(8,128)}, u32[]{:S(2)}, u32[]{:S(2)}) %collective-permute-start.1) | collective-permute-done | bytes 3145760 | tf_op jit(solution)/shard_map/ppermute | solution.py:19
  234.1 24.7 %fusion.2 = f32[1,384,2048]{2,1,0:T(8,128)} fusion(f32[1,384,2048]{2,1,0:T(8,128)} %collective-permute-done.1, f32[1,384,2048]{2,1,0:T(8,128)} %collective-permute-done, f32[1,384,2048]{2,1,0:T(8,128)S(1)} %copy-done.3, f32[1,2048,2049]{2,1,0:T(8,128)S(1)} %copy-done.2, pred[]{:T(512)S(6)} %eq.6, f32[1,384,2048]{2,1,0:T(8,128)S(1)} %copy-done, ...), kind=kOutput, calls=%fused_computation.7 | convolution fusion | flops 19333644288 | bytes 35651584 | tf_op jit(solution)/shard_map/dot_general | solution.py:59
  258.8 1.3 collective-permute-start.2
  260.1 31.5 %convolution_multiply_fusion = f32[2048,2048]{0,1:T(8,128)S(1)} fusion(f32[1,384,2048]{2,1,0:T(8,128)} %param.5, f32[1,384,2048]{2,1,0:T(8,128)} %param.8, f32[2048,384]{0,1:T(8,128)} %copy-done.1), kind=kOutput, calls=%fused_computation.4 | convolution fusion | flops 19332333568 | bytes 26214400 | tf_op jit(solution)/shard_map/dot_general | solution.py:69
  291.5 40.8 %collective-permute-done.2 = f32[1,384,2048]{2,1,0:T(8,128)} collective-permute-done((f32[1,384,2048]{2,1,0:T(8,128)}, f32[1,384,2048]{2,1,0:T(8,128)}, u32[]{:S(2)}, u32[]{:S(2)}) %collective-permute-start.2) | collective-permute-done | bytes 3145760 | tf_op jit(solution)/shard_map/ppermute | solution.py:19
  332.4 9.5 %fusion.3 = (f32[1,384,2048]{2,1,0:T(8,128)}, f32[1,384,2048]{2,1,0:T(8,128)}, f32[2048]{0:T(1024)S(1)}) fusion(f32[1,384,2048]{2,1,0:T(8,128)} %param.9, f32[1,384,2048]{2,1,0:T(8,128)} %collective-permute-done.2, f32[2048,384]{0,1:T(8,128)} %copy-done.1, pred[]{:T(512)S(6)} %eq.7, f32[1,384,2048]{2,1,0:T(8,128)} %param.8), kind=kLoop, calls=%fused_computation.8 | loop fusion | flops 8648704 | bytes 18882560 | tf_op jit(solution)/shard_map/broadcast_in_dim | solution.py:79
  341.9 6.2 %pad_maximum_fusion = f32[2048,2049]{0,1:T(8,128)} fusion(f32[2048,1]{0,1:T(1,128)S(1)} %bitcast.88, f32[2048,2048]{0,1:T(8,128)S(1)} %convolution_multiply_fusion), kind=kLoop, calls=%fused_computation | loop fusion | flops 4196352 | bytes 33570816 | tf_op jit(solution)/shard_map/concatenate | solution.py:34
  348.1 0.0 reduce-scatter.2.cloned.1.call-update
  348.1 1.2 copy-done.4
  349.3 0.3 copy.14
  349.7 185.3 %reduce-scatter.2.cloned.1.call-done = f32[128,2049]{0,1:T(8,128)} async-done(((f32[2048,2049]{0,1:T(8,128)}), f32[128,2049]{0,1:T(8,128)}) %reduce-scatter.2.cloned.1.call-update) | async-done | bytes 1049104 | tf_op jit(solution)/shard_map/reduce_scatter | solution.py:37
  535.0 1.3 fusion.15
  536.3 1.3 copy.15
  537.6 1.2 fusion.17
  (12 shorter events, 0.0 us)
Async XLA Ops:
  7.2 10.0 %copy-start = (f32[1,384,2048]{2,1,0:T(8,128)S(1)}, f32[1,384,2048]{2,1,0:T(8,128)}, u32[]{:S(2)}) copy-start(f32[1,384,2048]{2,1,0:T(8,128)} %param.8) | copy-start | bytes 9437188
  7.2 185.9 %all-gather.2.cloned.1.call-start = ((), (), s32[]{:S(2)}) async-start(), calls=%async_computation.1 | async-start | bytes 18939904 | tf_op jit(solution)/shard_map/all_gather | solution.py:27
  10.5 524.5 %reduce-scatter.2.cloned.1.call-start = ((), (), s32[]{:S(2)}) async-start(), calls=%async_computation.2 | async-start | bytes 17895424 | tf_op jit(solution)/shard_map/reduce_scatter | solution.py:37
  10.5 208.3 %collective-permute-start = (f32[1,384,2048]{2,1,0:T(8,128)}, f32[1,384,2048]{2,1,0:T(8,128)}, u32[]{:S(2)}, u32[]{:S(2)}) collective-permute-start(f32[1,384,2048]{2,1,0:T(8,128)} %param.9), channel_id=1, source_target_pairs={{0,16},{16,32},{32,48},{48,64},{64,80},{80,96},{96,112},{1,17},{17... | collective-permute-start | bytes 9437192 | tf_op jit(solution)/shard_map/ppermute | solution.py:19
  17.2 216.9 %collective-permute-start.1 = (f32[1,384,2048]{2,1,0:T(8,128)S(1)}, f32[1,384,2048]{2,1,0:T(8,128)}, u32[]{:S(2)}, u32[]{:S(2)}) collective-permute-start(f32[1,384,2048]{2,1,0:T(8,128)S(1)} %copy-done), channel_id=1, source_target_pairs={{0,16},{16,32},{32,48},{48,64},{64,80},{80,96},{96,112},{1,17},{17... | collective-permute-start | bytes 9437192 | tf_op jit(solution)/shard_map/ppermute | solution.py:19
  194.7 39.4 %copy-start.2 = (f32[1,2048,2049]{2,1,0:T(8,128)S(1)}, f32[1,2048,2049]{2,1,0:T(8,128)}, u32[]{:S(2)}) copy-start(f32[1,2048,2049]{2,1,0:T(8,128)} %all-gather.2.cloned.1.call-done) | copy-start | bytes 50356228
  194.7 39.4 %copy-start.3 = (f32[1,384,2048]{2,1,0:T(8,128)S(1)}, f32[1,384,2048]{2,1,0:T(8,128)}, u32[]{:S(2)}) copy-start(f32[1,384,2048]{2,1,0:T(8,128)} %param.5) | copy-start | bytes 9437188
  218.8 40.0 %copy-start.1 = (f32[2048,384]{0,1:T(8,128)}, f32[2048,384]{0,1:T(8,128)S(1)}, u32[]{:S(2)}) copy-start(f32[2048,384]{0,1:T(8,128)S(1)} %multiply_add_fusion) | copy-start | bytes 9437188
  258.8 73.6 %collective-permute-start.2 = (f32[1,384,2048]{2,1,0:T(8,128)}, f32[1,384,2048]{2,1,0:T(8,128)}, u32[]{:S(2)}, u32[]{:S(2)}) collective-permute-start(f32[1,384,2048]{2,1,0:T(8,128)} %fusion.2), channel_id=1, source_target_pairs={{16,0},{32,16},{48,32},{64,48},{80,64},{96,80},{112,96},{17,1},{33... | collective-permute-start | bytes 9437192 | tf_op jit(solution)/shard_map/ppermute | solution.py:19
  348.1 1.2 copy-start.4
  349.6 188.0 %copy-start.5 = (f32[1,128]{1,0:T(1,128)S(1)}, f32[1,128]{1,0:T(1,128)}, u32[]{:S(2)}) copy-start(f32[1,128]{1,0:T(1,128)} %param.7) | copy-start | bytes 1540
Sparse Core Ops, SparseCore 0:
  10.6 182.4 all-gather.1
  348.2 186.6 reduce-scatter.1
where the time goes:
time: 546 us
  waiting for transfers between devices  414 us (76%)
  matrix products  80.2 us (15%)
  other arithmetic  20.6 us (4%)
  between operations  14.1 us (3%)
  starting transfers between devices  11.8 us (2%)
    reduce_scatter x1, waiting for transfers between devices, in_one_piece(): out = lax.psum_scatter(both, axis, scatter_dimension=dim, tiled=True)  185 us
    all_gather x1, waiting for transfers between devices, side_by_side(): out = lax.all_gather(both, axis, axis=dim, tiled=True)  172 us
    ppermute x3, waiting for transfers between devices, passed_along(): return lax.ppermute(block, axis, route)  56.1 us
    dot_general x1, matrix products, body(): jnp.dot(misfit.T, inputs_here, precision=highest)  31.5 us
    dot_general x1, matrix products, body(): pulled = scaling * jnp.dot(misfit, whole_weight[0], precision=highest)  24.7 us
    dot_general x1, matrix products, body(): jnp.dot(inputs_here, whole_weight[0].T, precision=highest)  24.1 us
    ppermute x3, starting transfers between devices, passed_along(): return lax.ppermute(block, axis, route)  11.7 us
  transfers between devices with their start and end apart: 5, of which 4 were waited for; matrix products, arithmetic and copies ran while one was open for 11% of the time, Pallas kernels for 0%

commit v1 on v0

v1 whole, which is shorter than its diff:
```python
import functools
import math

import jax
import jax.numpy as jnp
from jax import lax
from jax.experimental import pallas as pl
from jax.experimental.pallas import tpu as pltpu
from jax.sharding import PartitionSpec as P

D = 2048
BLOCK = 128
PAIR = 2 * BLOCK
QUAD = 4 * BLOCK
TAU_P = 0.5
TILES = 2
WIDE = 512
SMALL = pl.CostEstimate(flops=1024, bytes_accessed=1024, transcendentals=0)


def dp_move(v, step):
    return lax.ppermute(v, "dp", [(i, step(i)) for i in range(16)])


def core_swap(v):
    return dp_move(v, lambda i: i ^ 1)


def x_swap(v):
    return dp_move(v, lambda i: i ^ 2)


def y_shift(v, k):
    return dp_move(v, lambda i: (i + 4 * k) % 16)


def depth_shift(v, k):
    n = lax.axis_size("depth")
    return lax.ppermute(v, "depth", [(i, i + k) for i in range(n) if 0 <= i + k < n])


def after(v, *deps):
    return lax.optimization_barrier((v, *deps))[0]


def parity_kernel(s_ref, x_ref, mine_ref, theirs_ref):
    first_x, even = s_ref[1] == 0, s_ref[2] == 0
    tiles = [x_ref[:, n * BLOCK : (n + 1) * BLOCK] for n in range(4)]
    for pos in range(2):
        cols = slice(pos * BLOCK, (pos + 1) * BLOCK)
        a = jnp.where(first_x, tiles[2 * pos], tiles[2 - 2 * pos])
        b = jnp.where(first_x, tiles[2 * pos + 1], tiles[3 - 2 * pos])
        mine_ref[:, cols] = jnp.where(even, a, b)
        theirs_ref[:, cols] = jnp.where(even, b, a)


def split_parity(place, v):
    rows = v.shape[0]
    half = jax.ShapeDtypeStruct((4, rows, PAIR), v.dtype)
    return pl.pallas_call(
        parity_kernel,
        out_shape=(half, half),
        grid_spec=pltpu.PrefetchScalarGridSpec(
            num_scalar_prefetch=1,
            grid=(4,),
            in_specs=[pl.BlockSpec((rows, QUAD), lambda k, s: (0, lax.rem(s[0] + k, 4)))],
            out_specs=[pl.BlockSpec((None, rows, PAIR), lambda k, s: (k, 0, 0))] * 2,
        ),
        cost_estimate=SMALL,
        name="parity",
    )(place, v)


def last_kernel(s_ref, mine_ref, theirs_ref, r_ref, q_ref, u_ref, qo_ref, uo_ref):
    first_x, even, is_last = s_ref[1] == 0, s_ref[2] == 0, s_ref[3] == 1
    mine = [mine_ref[:, :BLOCK], mine_ref[:, BLOCK:]]
    theirs = [theirs_ref[:, :BLOCK], theirs_ref[:, BLOCK:]]
    for xx in range(2):
        a = jnp.where(first_x, mine[xx], mine[1 - xx])
        b = jnp.where(first_x, theirs[xx], theirs[1 - xx])
        for cc, affine in enumerate((jnp.where(even, a, b), jnp.where(even, b, a))):
            n = 2 * xx + cc
            cols = slice(n * BLOCK, (n + 1) * BLOCK)
            q, u = q_ref[:, cols], u_ref[:, cols]
            nxt = r_ref[:, cols] - TAU_P * (u - q)
            coupled = jnp.maximum(0.0, (affine + nxt + u) * 0.5)
            q_new = jnp.where(is_last, jnp.maximum(0.0, affine), coupled)
            qo_ref[:, cols] = q_new
            uo_ref[:, cols] = jnp.where(is_last, u, u + (nxt - q_new))


def last_step(part, parts, place, mine, theirs, r, q, u, so_far):
    rows = q.shape[0] // parts
    half = pl.BlockSpec((None, rows, PAIR), lambda g, s: (lax.rem(g + 4 - s[0], 4), part, 0))
    full = pl.BlockSpec((rows, QUAD), lambda g, s: (part, g))
    out = jax.ShapeDtypeStruct(q.shape, jnp.float32)
    left = pl.BlockSpec(memory_space=pl.ANY)
    kernel = last_kernel if so_far is None else lambda *refs: last_kernel(*refs[:6], *refs[8:])
    more = () if so_far is None else so_far
    return pl.pallas_call(
        kernel,
        out_shape=(out, out),
        grid_spec=pltpu.PrefetchScalarGridSpec(
            num_scalar_prefetch=1,
            grid=(4,),
            in_specs=[half, half, pl.BlockSpec((rows, QUAD), lambda g, s: (0, g)), full, full]
            + [left] * len(more),
            out_specs=[full, full],
        ),
        input_output_aliases={6 + n: n for n in range(len(more))},
        cost_estimate=SMALL,
        name="last_step",
    )(place, mine, theirs, r, q, u, *more)


def dot(a, b, left, right):
    return lax.dot_general(a, b, (((left,), (right,)), ((), ())), preferred_element_type=jnp.float32)


def split(v):
    hi = v.astype(jnp.bfloat16)
    return hi, (v - hi.astype(jnp.float32)).astype(jnp.bfloat16)


def step_kernel(blocks, n_bias, first, apart, ph_ref, pl_ref, *refs):
    n = len(blocks)
    w_refs, q_refs, b_refs = refs[:n], refs[n : 2 * n], refs[2 * n : 2 * n + n_bias]
    refs = refs[2 * n + n_bias :]
    if not first:
        old_ref, refs = refs[0], refs[1:]
    outs, refs = refs[: 1 + apart], refs[1 + apart :]
    aff_ref, refs = refs[0], refs[1:]
    g_refs, (wh, wl, sum_ref) = refs[:n], refs[n:]
    scaling = 1.0 / math.sqrt(D)
    r = pl.program_id(0)

    @pl.when(r == 0)
    def _():
        for j, w_ref in enumerate(w_refs):
            at = slice(j * BLOCK, (j + 1) * BLOCK)
            wh[at, :], wl[at, :] = split(w_ref[...])
        for g_ref in g_refs:
            g_ref[...] = jnp.zeros_like(g_ref)
        sum_ref[...] = jnp.zeros_like(sum_ref)

    ph, plo = ph_ref[...], pl_ref[...]
    product = dot(ph, wh[...], 1, 1) + (dot(ph, wl[...], 1, 1) + dot(plo, wh[...], 1, 1))
    shift = jnp.concatenate([b_refs[a][row : row + 1, :] for a, row in blocks], axis=1)
    affine = scaling * product + shift
    aff_ref[...] = affine
    misfit = affine - jnp.concatenate([q_ref[...] for q_ref in q_refs], axis=1)
    sum_ref[...] += jnp.sum(misfit, axis=0, keepdims=True)
    mh, ml = split(misfit)

    def chunk(step, _):
        cols = pl.ds(pl.multiple_of(step * WIDE, WIDE), WIDE)
        back = dot(mh, wh[:, cols], 1, 0) + (dot(mh, wl[:, cols], 1, 0) + dot(ml, wh[:, cols], 1, 0))
        if not first:
            back += old_ref[:, cols]
        for k, out_ref in enumerate(outs):
            if apart:

                @pl.when(r == k)
                def _():
                    out_ref[:, cols] = back
            else:
                out_ref[:, cols] = back
        grad = dot(mh, ph_ref[:, cols], 0, 0) + (dot(mh, pl_ref[:, cols], 0, 0) + dot(ml, ph_ref[:, cols], 0, 0))
        for j, g_ref in enumerate(g_refs):
            g_ref[:BLOCK, cols] += grad[j * BLOCK : (j + 1) * BLOCK]

    lax.fori_loop(0, D // WIDE, chunk, None)

    @pl.when(r == TILES - 1)
    def _():
        for j, g_ref in enumerate(g_refs):
            g_ref[BLOCK : BLOCK + 1, :BLOCK] = sum_ref[:, j * BLOCK : (j + 1) * BLOCK]


def layer_step(blocks, ph, plo, qs, biases, old, apart=False):
    rows = ph.shape[0]
    tile, n = rows // TILES, len(blocks)
    first = old is None
    by_tile = pl.BlockSpec((tile, D), lambda r: (r, 0))
    fixed = lambda *shape: pl.BlockSpec(shape, lambda r: (0, 0))
    weight_blocks = [w for w, _, _ in blocks]
    targets = [
        pl.BlockSpec((None, tile, BLOCK), functools.partial(lambda k, pos, r: (k, r, pos), *at))
        for _, _, at in blocks
    ]
    args = [ph, plo, *weight_blocks, *[qs] * n, *biases]
    specs = [by_tile, by_tile, *[fixed(BLOCK, D)] * n, *targets, *[fixed(2, BLOCK)] * len(biases)]
    aliases = {}
    if not first:
        args.append(old)
        specs.append(by_tile)
        if not apart:
            aliases = {len(args) - 1: 0}
    f32 = lambda *shape: jax.ShapeDtypeStruct(shape, jnp.float32)
    kernel = functools.partial(step_kernel, [b for _, b, _ in blocks], len(biases), first, apart)
    pulled_shapes = [f32(tile, D)] * 2 if apart else [f32(rows, D)]
    pulled_specs = [fixed(tile, D)] * 2 if apart else [by_tile]
    out = pl.pallas_call(
        kernel,
        grid=(TILES,),
        out_shape=(*pulled_shapes, f32(rows, n * BLOCK), *[f32(BLOCK + 8, D)] * n),
        in_specs=specs,
        out_specs=(
            *pulled_specs,
            pl.BlockSpec((tile, n * BLOCK), lambda r: (r, 0)),
            *[fixed(BLOCK + 8, D)] * n,
        ),
        scratch_shapes=[
            pltpu.VMEM((n * BLOCK, D), jnp.bfloat16),
            pltpu.VMEM((n * BLOCK, D), jnp.bfloat16),
            pltpu.VMEM((1, n * BLOCK), jnp.float32),
        ],
        input_output_aliases=aliases,
        compiler_params=pltpu.CompilerParams(vmem_limit_bytes=58 << 20),
        cost_estimate=SMALL,
        name="layer_step",
    )(*args)
    k = len(pulled_shapes)
    return (out[:k] if apart else out[0]), out[k], out[k + 1 :]


def body(layer_inputs, weights, offsets, layer_outputs, multipliers):
    scaling = 1.0 / math.sqrt(D)
    p, q, u, w = layer_inputs[0], layer_outputs[0], multipliers[0], weights[0]
    rows = p.shape[0]
    samples = rows * lax.axis_size("dp")
    step_weight = 8.0 / math.sqrt(samples)
    step_offset = 0.5 / math.sqrt(samples)
    layer = lax.axis_index("depth")
    last = lax.axis_size("depth") - 1
    me = lax.axis_index("dp")
    y, x, core = me // 4, (me // 2) % 2, me % 2
    place = jnp.stack([y, x, core, layer == last]).astype(jnp.int32)

    hold = lax.optimization_barrier
    third = rows // 3
    thirds = [slice(n * third, (n + 1) * third) for n in range(3)]

    w_x = x_swap(w)
    w_up, w_down = y_shift(w, 1), y_shift(w, -1)
    p_other = core_swap(p)
    q_mine, q_theirs = split_parity(place, q)
    q_other = core_swap(q_theirs)
    b_pair = jnp.concatenate([offsets, x_swap(offsets)], axis=0)
    ahead = [u[t] - q[t] for t in thirds]
    w_x, w_up, w_down, p_other, q_other, q_mine, b_pair, ahead = hold(
        (w_x, w_up, w_down, p_other, q_other, q_mine, b_pair, ahead)
    )
    w_far, wx_down = y_shift(w_up, 1), y_shift(w_x, -1)
    s0 = depth_shift(ahead[0], 1)
    b_up, b_down, b_far = (y_shift(b_pair, k) for k in (1, -1, 2))
    both = jnp.concatenate([p, p_other], axis=0)
    p_top = lax.reduce_precision(both, exponent_bits=8, mantissa_bits=7)
    ph, plo = p_top.astype(jnp.bfloat16), (both - p_top).astype(jnp.bfloat16)
    qs = jnp.concatenate([q_mine, q_other], axis=1)
    blocks = [(w, (0, 0), (0, 0)), (w_x, (0, 1), (0, 1))]
    pulled, a_own, (g_own, g_own_x) = layer_step(blocks, ph, plo, qs, [b_pair], None)
    w_far, wx_down, s0, b_up, b_down, b_far, ph, plo, qs, pulled, a_own, g_own, g_own_x = hold(
        (w_far, wx_down, s0, b_up, b_down, b_far, ph, plo, qs, pulled, a_own, g_own, g_own_x)
    )
    wx_up, wx_far = y_shift(w_x, 1), y_shift(wx_down, -1)
    s1 = depth_shift(after(ahead[1], s0), 1)
    blocks = [
        (w_up, (0, 0), (3, 0)),
        (w_down, (1, 0), (1, 0)),
        (w_far, (2, 0), (2, 0)),
        (wx_down, (1, 1), (1, 1)),
    ]
    biases = [b_up, b_down, b_far]
    pulled, a_some, (g_lo, g_hi, g_far, g_hi_x) = layer_step(blocks, ph, plo, qs, biases, pulled)
    wx_up, wx_far, s1, a_some, pulled, g_lo, g_hi, g_far, g_hi_x = hold(
        (wx_up, wx_far, s1, a_some, pulled, g_lo, g_hi, g_far, g_hi_x)
    )
    far_below, down = y_shift(g_far, 1), y_shift(g_lo, -1)
    s2 = depth_shift(after(ahead[2], s1), 1)
    blocks = [(wx_up, (0, 1), (3, 1)), (wx_far, (1, 1), (2, 1))]
    (ours, theirs), a_rest, (g_lo_x, g_far_x) = layer_step(
        blocks, ph, plo, qs, [b_up, b_far], pulled, apart=True
    )
    pulled_other = core_swap(theirs)
    r = [p[t] - TAU_P * (scaling * (ours[t] + pulled_other[t]) + p[t]) for t in thirds]
    far_below, down, s2, g_lo_x, g_far_x, r, a_rest = hold((far_below, down, s2, g_lo_x, g_far_x, r, a_rest))
    up_x, far_above = y_shift(g_hi_x, 1), y_shift(g_far_x, -1)
    r0 = depth_shift(r[0], -1)
    columns = [
        (a_own[:, :BLOCK], a_own[:, BLOCK:]),
        (a_some[:, BLOCK : 2 * BLOCK], a_some[:, 3 * BLOCK :]),
        (a_some[:, 2 * BLOCK : 3 * BLOCK], a_rest[:, BLOCK:]),
        (a_some[:, :BLOCK], a_rest[:, :BLOCK]),
    ]
    affine = jnp.stack([jnp.concatenate(pair, axis=1) for pair in columns])
    affine_other = core_swap(affine[:, rows:])
    hi_sum = g_hi + far_below
    own_sum = g_own + down
    moved = jnp.concatenate([a - TAU_P * b for a, b in zip(r, (s0, s1, s2))], axis=0)
    inputs_new = jnp.where(layer == 0, p, moved)
    up_x, far_above, r0, affine_mine, affine_other, hi_sum, own_sum, inputs_new, r = hold(
        (up_x, far_above, r0, affine[:, :rows], affine_other, hi_sum, own_sum, inputs_new, r)
    )
    up, down_x = y_shift(hi_sum, 1), y_shift(g_lo_x + far_above, -1)
    r1 = depth_shift(r[1], -1)
    args = (place, affine_mine, affine_other)
    out = last_step(0, 3, *args, r0, q, u, None)
    x_sum = g_own_x + up_x
    up, down_x, r1, out, x_sum, r = hold((up, down_x, r1, out, x_sum, r))
    from_x = x_swap(x_sum + down_x)
    r2 = depth_shift(r[2], -1)
    out = last_step(1, 3, *args, r1, q, u, out)
    own_sum = own_sum + up
    from_x, r2, out, own_sum = hold((from_x, r2, out, own_sum))
    outputs_new, mults_new = last_step(2, 3, *args, r2, q, u, out)
    grad = own_sum + from_x
    weights_new = w - (step_weight * scaling) * grad[:BLOCK]
    offsets_new = offsets - step_offset * grad[BLOCK : BLOCK + 1, :BLOCK]
    return (inputs_new[None], weights_new[None], offsets_new, outputs_new[None], mults_new[None])


def solution(mesh):
    three, two = P("depth", "dp", None), P("depth", "dp")
    specs = (three, three, two, three, three)
    return jax.shard_map(body, mesh=mesh, in_specs=specs, out_specs=specs, check_vma=False)
```

time: 546 us -> 293 us (0.54)
  waiting for transfers between devices: 414 us -> 122 us
  Pallas kernels: 0 us -> 83.6 us
  matrix products: 80.2 us -> 0 us
  starting transfers between devices: 11.8 us -> 45.9 us
  between operations: 14.1 us -> 1.18 us
  other arithmetic: 20.6 us -> 31.9 us
    reduce_scatter x1 -> x0, waiting for transfers between devices: 185 us -> none  [in_one_piece(): out = lax.psum_scatter(both, axis, scatter_dimension=dim, tiled=True)]
    all_gather x1 -> x0, waiting for transfers between devices: 172 us -> none  [side_by_side(): out = lax.all_gather(both, axis, axis=dim, tiled=True)]
    pallas_call x0 -> x7, Pallas kernels: none -> 83.6 us  [the longest x3 63.2 us: layer_step(): pl.pallas_call(kernel, grid=(TILES,), out_shape=(*pulled_shapes, f32(rows...]
    dot_general x3 -> x0, matrix products: 80.2 us -> none  [the longest x1 31.5 us: body(): jnp.dot(misfit.T, inputs_here, precision=highest)]
    ppermute x3 -> x28, waiting for transfers between devices: 56.1 us -> 122 us  [the longest x6 88.1 us: depth_shift(): lax.ppermute(v, 'depth', [(i, i + k) for i in range(n) if 0 <= i + k < n])]
    ppermute x3 -> x28, starting transfers between devices: 11.7 us -> 45.9 us  [the longest x22 27.2 us: dp_move(): return lax.ppermute(v, 'dp', [(i, step(i)) for i in range(16)])]
    add x0 -> x7, other arithmetic: none -> 10.5 us  [the longest x1 2.4 us: body(): own_sum = g_own + down]
    sub x2 -> x5, other arithmetic: 2.53 us -> 11.1 us  [the longest x1 4.88 us: body(): p[t] - TAU_P * (scaling * (ours[t] + pulled_other[t]) + p[t])]
  transfers between devices with their start and end apart: 5 -> 28, of which waited for: 4 -> 9; matrix products, arithmetic and copies ran while one was open for 11% -> 10% of each run, Pallas kernels for 0% -> 20%
where the time goes in v1:
time: 293 us; the launch traced here: 292 us
  waiting for transfers between devices  122 us (42%)
  Pallas kernels  83.6 us (29%)
  starting transfers between devices  45.9 us (16%)
  other arithmetic  31.9 us (11%)
  local copies, waits for them, and re-layouts  7.27 us (2%)
    ppermute x6, waiting for transfers between devices, depth_shift(): lax.ppermute(v, 'depth', [(i, i + k) for i in range(n) if 0 <= i + k < n])  88.1 us
    pallas_call x3, Pallas kernels, layer_step(): pl.pallas_call(kernel, grid=(TILES,), out_shape=(*pulled_shapes, f32(rows...  63.2 us
    ppermute x22, waiting for transfers between devices, dp_move(): return lax.ppermute(v, 'dp', [(i, step(i)) for i in range(16)])  33.9 us
    ppermute x22, starting transfers between devices, dp_move(): return lax.ppermute(v, 'dp', [(i, step(i)) for i in range(16)])  27.2 us
    ppermute x6, starting transfers between devices, depth_shift(): lax.ppermute(v, 'depth', [(i, i + k) for i in range(n) if 0 <= i + k < n])  18.7 us
    pallas_call x3, Pallas kernels, last_step(): pl.pallas_call(kernel, out_shape=(out, out), grid_spec=pltpu.PrefetchScal...  15.3 us
    convert_element_type x1, other arithmetic, body(): ph, plo = (p_top.astype(jnp.bfloat16), (both - p_top).astype(jnp.bfloat16))  5.96 us
  transfers between devices with their start and end apart: 28, of which 9 were waited for; matrix products, arithmetic and copies ran while one was open for 10% of the time, Pallas kernels for 20%

profile of v1, /device:TPU:0, one launch (start us, length us, event | category | flops | bytes accessed | tf_op | source)
XLA Modules:
  0.0 291.8 jit_solution(17608044787111082145)
XLA Ops:
  1.4 5.1 %parity.1 = (f32[4,384,256]{2,1,0:T(8,128)}, f32[4,384,256]{2,1,0:T(8,128)}) custom-call(s32[4]{0:T(128)} %pad_add_fusion.s_ref.refs_0_, f32[384,2048]{1,0:T(8,128)} %bitcast.34), custom_call_target="tpu_custom_call" | custom-call | flops 1024 | bytes 1024 | tf_op jit(solution)/shard_map/parity/pallas_call | solution.py:60
  10.5 2.9 %collective-permute-start.2 = (f32[128,2048]{1,0:T(8,128)}, f32[128,2048]{1,0:T(8,128)S(1)}, u32[]{:S(2)}, u32[]{:S(2)}) collective-permute-start(f32[128,2048]{1,0:T(8,128)} %bitcast.47), channel_id=1, source_target_pairs={{0,12},{1,13},{2,14},{3,15},{4,0},{5,1},{6,2},{7,3},{8,4},{9,5},{1... | collective-permute-start | bytes 3145736 | tf_op jit(solution)/shard_map/ppermute | solution.py:22
  13.4 3.7 %subtract_bitcast_fusion = (f32[128,2048]{1,0:T(8,128)}, f32[128,2048]{1,0:T(8,128)}, f32[128,2048]{1,0:T(8,128)}) fusion(f32[1,384,2048]{2,1,0:T(8,128)S(1)} %copy-done.1, f32[1,384,2048]{2,1,0:T(8,128)} %param.9), kind=kLoop, calls=%fused_computation.27 | loop fusion | flops 786432 | bytes 9437184 | tf_op jit(solution)/shard_map/sub | solution.py:250
  17.1 16.6 %collective-permute-done.refs_1_ = f32[128,2048]{1,0:T(8,128)} collective-permute-done((f32[128,2048]{1,0:T(8,128)}, f32[128,2048]{1,0:T(8,128)}, u32[]{:S(2)}, u32[]{:S(2)}) %collective-permute-start) | collective-permute-done | bytes 1048608 | tf_op jit(solution)/shard_map/ppermute | solution.py:22
  39.9 5.0 %collective-permute-start.9 = (f32[128,2048]{1,0:T(8,128)}, f32[128,2048]{1,0:T(8,128)S(1)}, u32[]{:S(2)}, u32[]{:S(2)}) collective-permute-start(f32[128,2048]{1,0:T(8,128)} %get-tuple-element.97), channel_id=1, source_target_pairs={{0,16},{16,32},{32,48},{48,64},{64,80},{80,96},{96,112},{1,17},{17... | collective-permute-start | bytes 3145736 | tf_op jit(solution)/shard_map/ppermute | solution.py:39
  45.0 3.2 %collective-permute-start.11 = (f32[2,128]{1,0:T(2,128)S(1)}, f32[2,128]{1,0:T(2,128)S(1)}, u32[]{:S(2)}, u32[]{:S(2)}) collective-permute-start(f32[2,128]{1,0:T(2,128)S(1)} %pad_maximum_fusion.2.refs_4_), channel_id=1, source_target_pairs={{0,12},{1,13},{2,14},{3,15},{4,0},{5,1},{6,2},{7,3},{8,4},{9,5},{1... | collective-permute-start | bytes 3080 | tf_op jit(solution)/shard_map/ppermute | solution.py:22
  48.2 6.0 %fusion = (bf16[768,2048]{1,0:T(8,128)(2,1)}, bf16[768,2048]{1,0:T(8,128)(2,1)}) fusion(f32[384,2048]{1,0:T(8,128)} %collective-permute-done.3, f32[384,2048]{1,0:T(8,128)S(1)} %bitcast.42), kind=kLoop, calls=%fused_computation.2 | loop fusion | flops 7864320 | bytes 12582912 | tf_op jit(solution)/shard_map/convert_element_type | solution.py:259
  54.3 7.4 %collective-permute-done.10.refs_8_.refs_4_ = f32[2,128]{1,0:T(2,128)S(1)} collective-permute-done((f32[2,128]{1,0:T(2,128)S(1)}, f32[2,128]{1,0:T(2,128)S(1)}, u32[]{:S(2)}, u32[]{:S(2)}) %collective-permute-start.10) | collective-permute-done | bytes 1056 | tf_op jit(solution)/shard_map/ppermute | solution.py:22
  64.5 16.1 %layer_step.3 = (f32[768,2048]{1,0:T(8,128)}, f32[768,256]{1,0:T(8,128)}, f32[136,2048]{1,0:T(8,128)}, f32[136,2048]{1,0:T(8,128)}) custom-call(bf16[768,2048]{1,0:T(8,128)(2,1)} %get-tuple-element.110.ph_ref, bf16[768,2048]{1,0:T(8,128)(2,1)} %get-tuple-element.111.pl_ref, f32[128,2048]{1,0:T(8,128)} %bitcast.48, f32[128,2048]{1,0:T(8,128)} %collective-permute-done.refs_1_, ...), custom_call_target="tpu_custom_call" | custom-call | flops 1024 | bytes 1024 | tf_op jit(solution)/shard_map/layer_step/pallas_call | solution.py:203
  82.3 5.0 %collective-permute-start.14 = (f32[128,2048]{1,0:T(8,128)S(1)}, f32[128,2048]{1,0:T(8,128)S(1)}, u32[]{:S(2)}, u32[]{:S(2)}) collective-permute-start(f32[128,2048]{1,0:T(8,128)S(1)} %copy-done.17), channel_id=1, source_target_pairs={{0,16},{16,32},{32,48},{48,64},{64,80},{80,96},{96,112},{1,17},{17... | collective-permute-start | bytes 3145736 | tf_op jit(solution)/shard_map/ppermute | solution.py:39
  89.2 27.3 %layer_step.4 = (f32[768,2048]{1,0:T(8,128)}, f32[768,512]{1,0:T(8,128)}, f32[136,2048]{1,0:T(8,128)}, f32[136,2048]{1,0:T(8,128)}, f32[136,2048]{1,0:T(8,128)}, /*index=5*/f32[136,2048]{1,0:T(8,128)}) custom-call(bf16[768,2048]{1,0:T(8,128)(2,1)} %get-tuple-element.110.ph_ref, ...), custom_call_target="tpu_custom_call", output_to_operand_aliasing={{0}: (13, {})} | custom-call | flops 1024 | bytes 1024 | tf_op jit(solution)/shard_map/layer_step/pallas_call | solution.py:203
  117.9 19.8 %layer_step.5 = (f32[384,2048]{1,0:T(8,128)}, f32[384,2048]{1,0:T(8,128)}, f32[768,256]{1,0:T(8,128)}, f32[136,2048]{1,0:T(8,128)}, f32[136,2048]{1,0:T(8,128)}) custom-call(bf16[768,2048]{1,0:T(8,128)(2,1)} %get-tuple-element.110.ph_ref, bf16[768,2048]{1,0:T(8,128)(2,1)} %get-tuple-element.111.pl_ref, f32[128,2048]{1,0:T(8,128)} %copy-done.22, ...), custom_call_target="tpu_custom_call" | custom-call | flops 1024 | bytes 1024 | tf_op jit(solution)/shard_map/layer_step/pallas_call | solution.py:203
  138.3 2.8 collective-permute-start.17
  141.1 4.7 %collective-permute-start.18 = (f32[128,2048]{1,0:T(8,128)}, f32[128,2048]{1,0:T(8,128)}, u32[]{:S(2)}, u32[]{:S(2)}) collective-permute-start(f32[128,2048]{1,0:T(8,128)} %get-tuple-element.130), channel_id=1, source_target_pairs={{0,16},{16,32},{32,48},{48,64},{64,80},{80,96},{96,112},{1,17},{17... | collective-permute-start | bytes 3145736 | tf_op jit(solution)/shard_map/ppermute | solution.py:39
  147.4 4.9 %fusion.6 = (f32[128,2048]{1,0:T(8,128)S(1)}, f32[128,2048]{1,0:T(8,128)}, f32[128,2048]{1,0:T(8,128)S(1)}) fusion(f32[384,2048]{1,0:T(8,128)} %collective-permute-done.19, f32[384,2048]{1,0:T(8,128)} %get-tuple-element.136, f32[1,384,2048]{2,1,0:T(8,128)S(1)} %copy-done.3), kind=kLoop, calls=%fused_computation.13 | loop fusion | flops 3932160 | bytes 12582912 | tf_op jit(solution)/shard_map/sub | solution.py:286
  152.3 15.3 %collective-permute-done.18 = f32[128,2048]{1,0:T(8,128)} collective-permute-done((f32[128,2048]{1,0:T(8,128)}, f32[128,2048]{1,0:T(8,128)}, u32[]{:S(2)}, u32[]{:S(2)}) %collective-permute-start.18) | collective-permute-done | bytes 1048608 | tf_op jit(solution)/shard_map/ppermute | solution.py:39
  172.9 2.4 add.57
  182.0 8.1 %collective-permute-done.15 = f32[136,2048]{1,0:T(8,128)S(1)} collective-permute-done((f32[136,2048]{1,0:T(8,128)}, f32[136,2048]{1,0:T(8,128)S(1)}, u32[]{:S(2)}, u32[]{:S(2)}) %collective-permute-start.15) | collective-permute-done | bytes 1114144 | tf_op jit(solution)/shard_map/ppermute | solution.py:22
  190.1 9.9 %collective-permute-done.21.r_ref = f32[128,2048]{1,0:T(8,128)S(1)} collective-permute-done((f32[128,2048]{1,0:T(8,128)S(1)}, f32[128,2048]{1,0:T(8,128)S(1)}, u32[]{:S(2)}, u32[]{:S(2)}) %collective-permute-start.21) | collective-permute-done | bytes 1048608 | tf_op jit(solution)/shard_map/ppermute | solution.py:39
  204.7 5.2 %last_step.3 = (f32[384,2048]{1,0:T(8,128)}, f32[384,2048]{1,0:T(8,128)}) custom-call(s32[4]{0:T(128)} %pad_add_fusion.s_ref.refs_0_, f32[4,384,256]{2,1,0:T(8,128)} %get-tuple-element.156.mine_ref.refs_1_, f32[4,384,256]{2,1,0:T(8,128)} %collective-permute-done.22.theirs_ref.refs_2_, f32[128,2048]{1,0:T(8,128)} %copy-done.21, f32[384,2048]{1,0:T(8,128)} %bitcast.35, ...), custom_call_target="tpu_custom_call" | custom-call | flops 1024 | bytes 1024 | tf_op jit(solution)/shard_map/last_step/pallas_call | solution.py:100
  210.0 21.1 %collective-permute-done.25.refs_3_ = f32[128,2048]{1,0:T(8,128)} collective-permute-done((f32[128,2048]{1,0:T(8,128)}, f32[128,2048]{1,0:T(8,128)}, u32[]{:S(2)}, u32[]{:S(2)}) %collective-permute-start.25) | collective-permute-done | bytes 1048608 | tf_op jit(solution)/shard_map/ppermute | solution.py:39
  235.4 5.0 %last_step.4 = (f32[384,2048]{1,0:T(8,128)}, f32[384,2048]{1,0:T(8,128)}) custom-call(s32[4]{0:T(128)} %pad_add_fusion.s_ref.refs_0_, f32[4,384,256]{2,1,0:T(8,128)} %get-tuple-element.156.mine_ref.refs_1_, f32[4,384,256]{2,1,0:T(8,128)} %collective-permute-done.22.theirs_ref.refs_2_, ...), custom_call_target="tpu_custom_call", output_to_operand_aliasing={{0}: (6, {}), {1}: (7, {})} | custom-call | flops 1024 | bytes 1024 | tf_op jit(solution)/shard_map/last_step/pallas_call | solution.py:100
  241.9 41.8 %collective-permute-done.27.refs_3_ = f32[128,2048]{1,0:T(8,128)} collective-permute-done((f32[128,2048]{1,0:T(8,128)S(1)}, f32[128,2048]{1,0:T(8,128)}, u32[]{:S(2)}, u32[]{:S(2)}) %collective-permute-start.27) | collective-permute-done | bytes 1048608 | tf_op jit(solution)/shard_map/ppermute | solution.py:39
  286.8 5.0 %last_step.5 = (f32[384,2048]{1,0:T(8,128)}, f32[384,2048]{1,0:T(8,128)}) custom-call(s32[4]{0:T(128)} %pad_add_fusion.s_ref.refs_0_, f32[4,384,256]{2,1,0:T(8,128)} %get-tuple-element.156.mine_ref.refs_1_, f32[4,384,256]{2,1,0:T(8,128)} %collective-permute-done.22.theirs_ref.refs_2_, ...), custom_call_target="tpu_custom_call", output_to_operand_aliasing={{0}: (6, {}), {1}: (7, {})} | custom-call | flops 1024 | bytes 1024 | tf_op jit(solution)/shard_map/last_step/pallas_call | solution.py:100
  (128 shorter events, 46.2 us)
Async XLA Ops:
  0.7 34.7 %collective-permute-start.3 = (f32[384,2048]{1,0:T(8,128)}, f32[384,2048]{1,0:T(8,128)}, u32[]{:S(2)}, u32[]{:S(2)}) collective-permute-start(f32[384,2048]{1,0:T(8,128)} %bitcast.41), channel_id=1, source_target_pairs={{0,1},{1,0},{2,3},{3,2},{4,5},{5,4},{6,7},{7,6},{8,9},{9,8},{10,11... | collective-permute-start | bytes 9437192 | tf_op jit(solution)/shard_map/ppermute | solution.py:22
  6.5 28.9 %collective-permute-start.4 = (f32[4,384,256]{2,1,0:T(8,128)}, f32[4,384,256]{2,1,0:T(8,128)S(1)}, u32[]{:S(2)}, u32[]{:S(2)}) collective-permute-start(f32[4,384,256]{2,1,0:T(8,128)} %get-tuple-element.93), channel_id=1, source_target_pairs={{0,1},{1,0},{2,3},{3,2},{4,5},{5,4},{6,7},{7,6},{8,9},{9,8},{10,11... | collective-permute-start | bytes 4718600 | tf_op jit(solution)/shard_map/ppermute | solution.py:22
  8.4 25.3 %collective-permute-start = (f32[128,2048]{1,0:T(8,128)}, f32[128,2048]{1,0:T(8,128)}, u32[]{:S(2)}, u32[]{:S(2)}) collective-permute-start(f32[128,2048]{1,0:T(8,128)} %bitcast.45), channel_id=1, source_target_pairs={{0,2},{1,3},{2,0},{3,1},{4,6},{5,7},{6,4},{7,5},{8,10},{9,11},{10,... | collective-permute-start | bytes 3145736 | tf_op jit(solution)/shard_map/ppermute | solution.py:22
  8.8 26.4 %collective-permute-start.1 = (f32[128,2048]{1,0:T(8,128)}, f32[128,2048]{1,0:T(8,128)}, u32[]{:S(2)}, u32[]{:S(2)}) collective-permute-start(f32[128,2048]{1,0:T(8,128)} %bitcast.46), channel_id=1, source_target_pairs={{0,4},{1,5},{2,6},{3,7},{4,8},{5,9},{6,10},{7,11},{8,12},{9,13},{1... | collective-permute-start | bytes 3145736 | tf_op jit(solution)/shard_map/ppermute | solution.py:22
  10.5 24.9 %collective-permute-start.2 = (f32[128,2048]{1,0:T(8,128)}, f32[128,2048]{1,0:T(8,128)S(1)}, u32[]{:S(2)}, u32[]{:S(2)}) collective-permute-start(f32[128,2048]{1,0:T(8,128)} %bitcast.47), channel_id=1, source_target_pairs={{0,12},{1,13},{2,14},{3,15},{4,0},{5,1},{6,2},{7,3},{8,4},{9,5},{1... | collective-permute-start | bytes 3145736 | tf_op jit(solution)/shard_map/ppermute | solution.py:22
  36.3 46.0 %collective-permute-start.7 = (f32[128,2048]{1,0:T(8,128)}, f32[128,2048]{1,0:T(8,128)}, u32[]{:S(2)}, u32[]{:S(2)}) collective-permute-start(f32[128,2048]{1,0:T(8,128)} %collective-permute-done.1.refs_0_), channel_id=1, source_target_pairs={{0,4},{1,5},{2,6},{3,7},{4,8},{5,9},{6,10},{7,11},{8,12},{9,13},{1... | collective-permute-start | bytes 3145736 | tf_op jit(solution)/shard_map/ppermute | solution.py:22
  37.6 44.7 %collective-permute-start.8 = (f32[128,2048]{1,0:T(8,128)}, f32[128,2048]{1,0:T(8,128)}, u32[]{:S(2)}, u32[]{:S(2)}) collective-permute-start(f32[128,2048]{1,0:T(8,128)} %collective-permute-done.refs_1_), channel_id=1, source_target_pairs={{0,12},{1,13},{2,14},{3,15},{4,0},{5,1},{6,2},{7,3},{8,4},{9,5},{1... | collective-permute-start | bytes 3145736 | tf_op jit(solution)/shard_map/ppermute | solution.py:22
  39.9 42.4 %collective-permute-start.9 = (f32[128,2048]{1,0:T(8,128)}, f32[128,2048]{1,0:T(8,128)S(1)}, u32[]{:S(2)}, u32[]{:S(2)}) collective-permute-start(f32[128,2048]{1,0:T(8,128)} %get-tuple-element.97), channel_id=1, source_target_pairs={{0,16},{16,32},{32,48},{48,64},{64,80},{80,96},{96,112},{1,17},{17... | collective-permute-start | bytes 3145736 | tf_op jit(solution)/shard_map/ppermute | solution.py:39
  45.0 35.6 %collective-permute-start.11 = (f32[2,128]{1,0:T(2,128)S(1)}, f32[2,128]{1,0:T(2,128)S(1)}, u32[]{:S(2)}, u32[]{:S(2)}) collective-permute-start(f32[2,128]{1,0:T(2,128)S(1)} %pad_maximum_fusion.2.refs_4_), channel_id=1, source_target_pairs={{0,12},{1,13},{2,14},{3,15},{4,0},{5,1},{6,2},{7,3},{8,4},{9,5},{1... | collective-permute-start | bytes 3080 | tf_op jit(solution)/shard_map/ppermute | solution.py:22
  80.6 36.0 %collective-permute-start.6 = (f32[128,2048]{1,0:T(8,128)}, f32[128,2048]{1,0:T(8,128)S(1)}, u32[]{:S(2)}, u32[]{:S(2)}) collective-permute-start(f32[128,2048]{1,0:T(8,128)} %collective-permute-done.refs_1_), channel_id=1, source_target_pairs={{0,4},{1,5},{2,6},{3,7},{4,8},{5,9},{6,10},{7,11},{8,12},{9,13},{1... | collective-permute-start | bytes 3145736 | tf_op jit(solution)/shard_map/ppermute | solution.py:22
  82.3 34.3 %collective-permute-start.14 = (f32[128,2048]{1,0:T(8,128)S(1)}, f32[128,2048]{1,0:T(8,128)S(1)}, u32[]{:S(2)}, u32[]{:S(2)}) collective-permute-start(f32[128,2048]{1,0:T(8,128)S(1)} %copy-done.17), channel_id=1, source_target_pairs={{0,16},{16,32},{32,48},{48,64},{64,80},{80,96},{96,112},{1,17},{17... | collective-permute-start | bytes 3145736 | tf_op jit(solution)/shard_map/ppermute | solution.py:39
  87.3 29.3 %collective-permute-start.13 = (f32[128,2048]{1,0:T(8,128)}, f32[128,2048]{1,0:T(8,128)S(1)}, u32[]{:S(2)}, u32[]{:S(2)}) collective-permute-start(f32[128,2048]{1,0:T(8,128)} %collective-permute-done.8.refs_3_), channel_id=1, source_target_pairs={{0,12},{1,13},{2,14},{3,15},{4,0},{5,1},{6,2},{7,3},{8,4},{9,5},{1... | collective-permute-start | bytes 3145736 | tf_op jit(solution)/shard_map/ppermute | solution.py:22
  137.8 29.8 %collective-permute-start.16 = (f32[136,2048]{1,0:T(8,128)}, f32[136,2048]{1,0:T(8,128)}, u32[]{:S(2)}, u32[]{:S(2)}) collective-permute-start(f32[136,2048]{1,0:T(8,128)} %get-tuple-element.126), channel_id=1, source_target_pairs={{0,4},{1,5},{2,6},{3,7},{4,8},{5,9},{6,10},{7,11},{8,12},{9,13},{1... | collective-permute-start | bytes 3342344 | tf_op jit(solution)/shard_map/ppermute | solution.py:22
  138.3 29.3 %collective-permute-start.17 = (f32[136,2048]{1,0:T(8,128)}, f32[136,2048]{1,0:T(8,128)}, u32[]{:S(2)}, u32[]{:S(2)}) collective-permute-start(f32[136,2048]{1,0:T(8,128)} %get-tuple-element.127), channel_id=1, source_target_pairs={{0,12},{1,13},{2,14},{3,15},{4,0},{5,1},{6,2},{7,3},{8,4},{9,5},{1... | collective-permute-start | bytes 3342344 | tf_op jit(solution)/shard_map/ppermute | solution.py:22
  141.1 26.5 %collective-permute-start.18 = (f32[128,2048]{1,0:T(8,128)}, f32[128,2048]{1,0:T(8,128)}, u32[]{:S(2)}, u32[]{:S(2)}) collective-permute-start(f32[128,2048]{1,0:T(8,128)} %get-tuple-element.130), channel_id=1, source_target_pairs={{0,16},{16,32},{32,48},{48,64},{64,80},{80,96},{96,112},{1,17},{17... | collective-permute-start | bytes 3145736 | tf_op jit(solution)/shard_map/ppermute | solution.py:39
  145.8 44.3 %collective-permute-start.15 = (f32[136,2048]{1,0:T(8,128)}, f32[136,2048]{1,0:T(8,128)S(1)}, u32[]{:S(2)}, u32[]{:S(2)}) collective-permute-start(f32[136,2048]{1,0:T(8,128)} %get-tuple-element.125), channel_id=1, source_target_pairs={{0,4},{1,5},{2,6},{3,7},{4,8},{5,9},{6,10},{7,11},{8,12},{9,13},{1... | collective-permute-start | bytes 3342344 | tf_op jit(solution)/shard_map/ppermute | solution.py:22
  169.6 30.4 %collective-permute-start.22 = (f32[4,384,256]{2,1,0:T(8,128)S(1)}, f32[4,384,256]{2,1,0:T(8,128)}, u32[]{:S(2)}, u32[]{:S(2)}) collective-permute-start(f32[4,384,256]{2,1,0:T(8,128)S(1)} %get-tuple-element.189), channel_id=1, source_target_pairs={{0,1},{1,0},{2,3},{3,2},{4,5},{5,4},{6,7},{7,6},{8,9},{9,8},{10,11... | collective-permute-start | bytes 4718600 | tf_op jit(solution)/shard_map/ppermute | solution.py:22
  169.7 30.4 %collective-permute-start.20 = (f32[136,2048]{1,0:T(8,128)S(1)}, f32[136,2048]{1,0:T(8,128)S(1)}, u32[]{:S(2)}, u32[]{:S(2)}) collective-permute-start(f32[136,2048]{1,0:T(8,128)S(1)} %copy-done.31), channel_id=1, source_target_pairs={{0,12},{1,13},{2,14},{3,15},{4,0},{5,1},{6,2},{7,3},{8,4},{9,5},{1... | collective-permute-start | bytes 3342344 | tf_op jit(solution)/shard_map/ppermute | solution.py:22
  171.4 28.6 %collective-permute-start.21 = (f32[128,2048]{1,0:T(8,128)S(1)}, f32[128,2048]{1,0:T(8,128)S(1)}, u32[]{:S(2)}, u32[]{:S(2)}) collective-permute-start(f32[128,2048]{1,0:T(8,128)S(1)} %get-tuple-element.140), channel_id=1, source_target_pairs={{16,0},{32,16},{48,32},{64,48},{80,64},{96,80},{112,96},{17,1},{33... | collective-permute-start | bytes 3145736 | tf_op jit(solution)/shard_map/ppermute | solution.py:39
  201.3 29.8 %collective-permute-start.24 = (f32[136,2048]{1,0:T(8,128)}, f32[136,2048]{1,0:T(8,128)}, u32[]{:S(2)}, u32[]{:S(2)}) collective-permute-start(f32[136,2048]{1,0:T(8,128)} %add.58), channel_id=1, source_target_pairs={{0,12},{1,13},{2,14},{3,15},{4,0},{5,1},{6,2},{7,3},{8,4},{9,5},{1... | collective-permute-start | bytes 3342344 | tf_op jit(solution)/shard_map/ppermute | solution.py:22
  201.6 29.5 %collective-permute-start.23 = (f32[136,2048]{1,0:T(8,128)}, f32[136,2048]{1,0:T(8,128)}, u32[]{:S(2)}, u32[]{:S(2)}) collective-permute-start(f32[136,2048]{1,0:T(8,128)} %add.56), channel_id=1, source_target_pairs={{0,4},{1,5},{2,6},{3,7},{4,8},{5,9},{6,10},{7,11},{8,12},{9,13},{1... | collective-permute-start | bytes 3342344 | tf_op jit(solution)/shard_map/ppermute | solution.py:22
  203.3 27.8 %collective-permute-start.25 = (f32[128,2048]{1,0:T(8,128)}, f32[128,2048]{1,0:T(8,128)}, u32[]{:S(2)}, u32[]{:S(2)}) collective-permute-start(f32[128,2048]{1,0:T(8,128)} %get-tuple-element.155), channel_id=1, source_target_pairs={{16,0},{32,16},{48,32},{64,48},{80,64},{96,80},{112,96},{17,1},{33... | collective-permute-start | bytes 3145736 | tf_op jit(solution)/shard_map/ppermute | solution.py:39
  232.5 51.2 %collective-permute-start.26 = (f32[136,2048]{1,0:T(8,128)S(1)}, f32[136,2048]{1,0:T(8,128)}, u32[]{:S(2)}, u32[]{:S(2)}) collective-permute-start(f32[136,2048]{1,0:T(8,128)S(1)} %add.60), channel_id=1, source_target_pairs={{0,2},{1,3},{2,0},{3,1},{4,6},{5,7},{6,4},{7,5},{8,10},{9,11},{10,... | collective-permute-start | bytes 3342344 | tf_op jit(solution)/shard_map/ppermute | solution.py:22
  234.1 49.6 %collective-permute-start.27 = (f32[128,2048]{1,0:T(8,128)S(1)}, f32[128,2048]{1,0:T(8,128)}, u32[]{:S(2)}, u32[]{:S(2)}) collective-permute-start(f32[128,2048]{1,0:T(8,128)S(1)} %copy-done.6), channel_id=1, source_target_pairs={{16,0},{32,16},{48,32},{64,48},{80,64},{96,80},{112,96},{17,1},{33... | collective-permute-start | bytes 3145736 | tf_op jit(solution)/shard_map/ppermute | solution.py:39
  (36 other events, 504.4 us)

commit v2 on v1

v2 whole, which is shorter than its diff:
```python
import functools
import math

import jax
import jax.numpy as jnp
from jax import lax
from jax.experimental import pallas as pl
from jax.experimental.pallas import tpu as pltpu
from jax.sharding import PartitionSpec as P

D = 2048
BLOCK = 128
PAIR = 2 * BLOCK
QUAD = 4 * BLOCK
TAU_P = 0.5
TILES = 2
EARLY_TILES = 4
WIDE = 512
SMALL = pl.CostEstimate(flops=1024, bytes_accessed=1024, transcendentals=0)


def dp_move(v, step):
    return lax.ppermute(v, "dp", [(i, step(i)) for i in range(16)])


def core_swap(v):
    return dp_move(v, lambda i: i ^ 1)


def x_swap(v):
    return dp_move(v, lambda i: i ^ 2)


def y_shift(v, k):
    return dp_move(v, lambda i: (i + 4 * k) % 16)


def depth_shift(v, k):
    n = lax.axis_size("depth")
    return lax.ppermute(v, "depth", [(i, i + k) for i in range(n) if 0 <= i + k < n])


def after(v, *deps):
    return lax.optimization_barrier((v, *deps))[0]


def parity_kernel(s_ref, x_ref, mine_ref, theirs_ref):
    first_x, even = s_ref[1] == 0, s_ref[2] == 0
    tiles = [x_ref[:, n * BLOCK : (n + 1) * BLOCK] for n in range(4)]
    for pos in range(2):
        cols = slice(pos * BLOCK, (pos + 1) * BLOCK)
        a = jnp.where(first_x, tiles[2 * pos], tiles[2 - 2 * pos])
        b = jnp.where(first_x, tiles[2 * pos + 1], tiles[3 - 2 * pos])
        mine_ref[:, cols] = jnp.where(even, a, b)
        theirs_ref[:, cols] = jnp.where(even, b, a)


def split_parity(place, v):
    rows = v.shape[0]
    half = jax.ShapeDtypeStruct((4, rows, PAIR), v.dtype)
    return pl.pallas_call(
        parity_kernel,
        out_shape=(half, half),
        grid_spec=pltpu.PrefetchScalarGridSpec(
            num_scalar_prefetch=1,
            grid=(4,),
            in_specs=[pl.BlockSpec((rows, QUAD), lambda k, s: (0, lax.rem(s[0] + k, 4)))],
            out_specs=[pl.BlockSpec((None, rows, PAIR), lambda k, s: (k, 0, 0))] * 2,
        ),
        cost_estimate=SMALL,
        name="parity",
    )(place, v)


def last_kernel(s_ref, mine_ref, theirs_ref, r_ref, q_ref, u_ref, *refs):
    qo_ref, uo_ref = refs[-2:]
    first_x, even, is_last = s_ref[1] == 0, s_ref[2] == 0, s_ref[3] == 1
    for g in range(4):
        k = lax.rem(g + 4 - s_ref[0], 4)
        mine = [mine_ref[k, :, :BLOCK], mine_ref[k, :, BLOCK:]]
        theirs = [theirs_ref[k, :, :BLOCK], theirs_ref[k, :, BLOCK:]]
        for xx in range(2):
            a = jnp.where(first_x, mine[xx], mine[1 - xx])
            b = jnp.where(first_x, theirs[xx], theirs[1 - xx])
            for cc, affine in enumerate((jnp.where(even, a, b), jnp.where(even, b, a))):
                n = 4 * g + 2 * xx + cc
                cols = slice(n * BLOCK, (n + 1) * BLOCK)
                q, u = q_ref[:, cols], u_ref[:, cols]
                nxt = r_ref[:, cols] - TAU_P * (u - q)
                coupled = jnp.maximum(0.0, (affine + nxt + u) * 0.5)
                q_new = jnp.where(is_last, jnp.maximum(0.0, affine), coupled)
                qo_ref[:, cols] = q_new
                uo_ref[:, cols] = jnp.where(is_last, u, u + (nxt - q_new))


def last_step(where, place, mine, theirs, r, q, u, so_far):
    rows = 64
    base = where.start // rows
    half = pl.BlockSpec((4, rows, PAIR), lambda i, s: (0, base + i, 0))
    full = pl.BlockSpec((rows, D), lambda i, s: (base + i, 0))
    out = jax.ShapeDtypeStruct(q.shape, jnp.float32)
    left = pl.BlockSpec(memory_space=pl.ANY)
    more = () if so_far is None else so_far
    return pl.pallas_call(
        last_kernel,
        out_shape=(out, out),
        grid_spec=pltpu.PrefetchScalarGridSpec(
            num_scalar_prefetch=1,
            grid=((where.stop - where.start) // rows,),
            in_specs=[half, half, pl.BlockSpec((rows, D), lambda i, s: (i, 0)), full, full]
            + [left] * len(more),
            out_specs=[full, full],
        ),
        input_output_aliases={6 + n: n for n in range(len(more))},
        cost_estimate=SMALL,
        name="last_step",
    )(place, mine, theirs, r, q, u, *more)


def dot(a, b, left, right):
    return lax.dot_general(a, b, (((left,), (right,)), ((), ())), preferred_element_type=jnp.float32)


def split(v):
    hi = v.astype(jnp.bfloat16)
    return hi, (v - hi.astype(jnp.float32)).astype(jnp.bfloat16)


def split_weights(w_refs, wh, wl):
    for j, w_ref in enumerate(w_refs):
        at = slice(j * BLOCK, (j + 1) * BLOCK)
        wh[at, :], wl[at, :] = split(w_ref[:BLOCK, :])


def affine_and_misfit(ph_ref, pl_ref, wh, wl, w_refs, q_refs, aff_ref, sum_ref):
    ph, plo = ph_ref[...], pl_ref[...]
    product = dot(ph, wh[...], 1, 1) + (dot(ph, wl[...], 1, 1) + dot(plo, wh[...], 1, 1))
    shift = jnp.concatenate([w_ref[BLOCK : BLOCK + 1, :BLOCK] for w_ref in w_refs], axis=1)
    affine = (1.0 / math.sqrt(D)) * product + shift
    aff_ref[...] = affine
    misfit = affine - jnp.concatenate([q_ref[...] for q_ref in q_refs], axis=1)
    sum_ref[...] += jnp.sum(misfit, axis=0, keepdims=True)
    return split(misfit)


def chunked(work):
    lax.fori_loop(0, D // WIDE, lambda n, _: work(pl.ds(pl.multiple_of(n * WIDE, WIDE), WIDE)), None)


def pulled_part(mh, ml, wh, wl, cols):
    return dot(mh, wh[:, cols], 1, 0) + (dot(mh, wl[:, cols], 1, 0) + dot(ml, wh[:, cols], 1, 0))


def add_gradient(mh, ml, ph_ref, pl_ref, g_refs, cols):
    grad = dot(mh, ph_ref[:, cols], 0, 0) + (dot(mh, pl_ref[:, cols], 0, 0) + dot(ml, ph_ref[:, cols], 0, 0))
    for j, g_ref in enumerate(g_refs):
        g_ref[:BLOCK, cols] += grad[j * BLOCK : (j + 1) * BLOCK]


def put_sums(sums, g_refs):
    for j, g_ref in enumerate(g_refs):
        g_ref[BLOCK : BLOCK + 1, :BLOCK] = sums[:, j * BLOCK : (j + 1) * BLOCK]


def step_kernel(n, first, ph_ref, pl_ref, *refs):
    w_refs, q_refs, refs = refs[:n], refs[n : 2 * n], refs[2 * n :]
    if not first:
        old_ref, refs = refs[0], refs[1:]
    out_ref, aff_ref, *refs = refs
    g_refs, (wh, wl, sum_ref) = refs[:n], refs[n:]
    r = pl.program_id(0)

    @pl.when(r == 0)
    def _():
        split_weights(w_refs, wh, wl)
        for g_ref in g_refs:
            g_ref[...] = jnp.zeros_like(g_ref)
        sum_ref[...] = jnp.zeros_like(sum_ref)

    mh, ml = affine_and_misfit(ph_ref, pl_ref, wh, wl, w_refs, q_refs, aff_ref, sum_ref)

    def work(cols):
        back = pulled_part(mh, ml, wh, wl, cols)
        out_ref[:, cols] = back if first else old_ref[:, cols] + back
        add_gradient(mh, ml, ph_ref, pl_ref, g_refs, cols)

    chunked(work)

    @pl.when(r == TILES - 1)
    def _():
        put_sums(sum_ref[...], g_refs)


def early_kernel(n, ph_ref, pl_ref, *refs):
    w_refs, q_refs, refs = refs[:n], refs[n : 2 * n], refs[2 * n :]
    old_ref, theirs_ref, ours_ref, aff_ref, mh_ref, ml_ref, sum_ref, wh, wl = refs
    r = pl.program_id(0)

    @pl.when(r == 0)
    def _():
        split_weights(w_refs, wh, wl)
        sum_ref[...] = jnp.zeros_like(sum_ref)

    mh, ml = affine_and_misfit(ph_ref, pl_ref, wh, wl, w_refs, q_refs, aff_ref, sum_ref)
    mh_ref[...], ml_ref[...] = mh, ml

    def work(cols):
        back = old_ref[:, cols] + pulled_part(mh, ml, wh, wl, cols)
        for k, out_ref in enumerate((theirs_ref, ours_ref)):

            @pl.when(r // (EARLY_TILES // 2) == k)
            def _():
                out_ref[:, cols] = back

    chunked(work)


def late_kernel(n, ph_ref, pl_ref, mh_ref, ml_ref, sum_ref, *g_refs):
    r = pl.program_id(0)

    @pl.when(r == 0)
    def _():
        for g_ref in g_refs:
            g_ref[...] = jnp.zeros_like(g_ref)

    mh, ml = mh_ref[...], ml_ref[...]
    chunked(lambda cols: add_gradient(mh, ml, ph_ref, pl_ref, g_refs, cols))

    @pl.when(r == TILES - 1)
    def _():
        put_sums(sum_ref[...], g_refs)


def f32(*shape):
    return jax.ShapeDtypeStruct(shape, jnp.float32)


def bf16(*shape):
    return jax.ShapeDtypeStruct(shape, jnp.bfloat16)


def fixed(*shape):
    return pl.BlockSpec(shape, lambda r: (0, 0))


def in_tiles(tiles, kernel, args, in_specs, out_shape, out_specs, scratch, aliases, name):
    return pl.pallas_call(
        kernel,
        grid=(tiles,),
        out_shape=tuple(out_shape),
        in_specs=in_specs,
        out_specs=tuple(out_specs),
        scratch_shapes=scratch,
        input_output_aliases=aliases,
        compiler_params=pltpu.CompilerParams(vmem_limit_bytes=(22 + 6 * len(out_shape)) << 20),
        cost_estimate=SMALL,
        name=name,
    )(*args)


def target_specs(blocks, tile, which):
    return [
        pl.BlockSpec((None, tile, BLOCK), functools.partial(lambda k, pos, r: (k, which(r), pos), *at))
        for _, at in blocks
    ]


def layer_step(blocks, ph, plo, qs, old):
    rows = ph.shape[0]
    tile, n = rows // TILES, len(blocks)
    by_tile = pl.BlockSpec((tile, D), lambda r: (r, 0))
    args = [ph, plo, *[w for w, _ in blocks], *[qs] * n]
    specs = [by_tile, by_tile, *[fixed(BLOCK + 8, D)] * n, *target_specs(blocks, tile, lambda r: r)]
    if old is not None:
        args.append(old)
        specs.append(by_tile)
    out = in_tiles(
        TILES,
        functools.partial(step_kernel, n, old is None),
        args,
        specs,
        [f32(rows, D), f32(rows, n * BLOCK), *[f32(BLOCK + 8, D)] * n],
        [by_tile, pl.BlockSpec((tile, n * BLOCK), lambda r: (r, 0)), *[fixed(BLOCK + 8, D)] * n],
        [
            pltpu.VMEM((n * BLOCK, D), jnp.bfloat16),
            pltpu.VMEM((n * BLOCK, D), jnp.bfloat16),
            pltpu.VMEM((1, n * BLOCK), jnp.float32),
        ],
        {} if old is None else {len(args) - 1: 0},
        "layer_step",
    )
    return out[0], out[1], out[2:]


def early_step(blocks, ph, plo, qs, old):
    rows = ph.shape[0]
    tile, n = rows // EARLY_TILES, len(blocks)
    half = EARLY_TILES // 2
    back = lambda r: lax.rem(r + half, EARLY_TILES)
    other_half = pl.BlockSpec((tile, D), lambda r: (jnp.minimum(r, half - 1), 0))
    own_half = pl.BlockSpec((tile, D), lambda r: (jnp.maximum(r - half, 0), 0))
    by_tile = lambda wide: pl.BlockSpec((tile, wide), lambda r: (back(r), 0))
    args = [ph, plo, *[w for w, _ in blocks], *[qs] * n, old]
    specs = [by_tile(D), by_tile(D), *[fixed(BLOCK + 8, D)] * n, *target_specs(blocks, tile, back)]
    specs.append(by_tile(D))
    wide = n * BLOCK
    return in_tiles(
        EARLY_TILES,
        functools.partial(early_kernel, n),
        args,
        specs,
        [f32(rows // 2, D), f32(rows // 2, D), f32(rows, wide), bf16(rows, wide), bf16(rows, wide), f32(1, wide)],
        [other_half, own_half, *[by_tile(wide)] * 3, fixed(1, wide)],
        [pltpu.VMEM((wide, D), jnp.bfloat16)] * 2,
        {},
        "early_step",
    )


def late_step(n, ph, plo, mh, ml, sums):
    rows = ph.shape[0]
    tile, wide = rows // TILES, n * BLOCK
    by_tile = lambda w: pl.BlockSpec((tile, w), lambda r: (r, 0))
    return in_tiles(
        TILES,
        functools.partial(late_kernel, n),
        [ph, plo, mh, ml, sums],
        [by_tile(D), by_tile(D), by_tile(wide), by_tile(wide), fixed(1, wide)],
        [f32(BLOCK + 8, D)] * n,
        [fixed(BLOCK + 8, D)] * n,
        [],
        {},
        "late_step",
    )


def body(layer_inputs, weights, offsets, layer_outputs, multipliers):
    scaling = 1.0 / math.sqrt(D)
    p, q, u, w = layer_inputs[0], layer_outputs[0], multipliers[0], weights[0]
    rows = p.shape[0]
    samples = rows * lax.axis_size("dp")
    step_weight = 8.0 / math.sqrt(samples)
    step_offset = 0.5 / math.sqrt(samples)
    layer = lax.axis_index("depth")
    last = lax.axis_size("depth") - 1
    me = lax.axis_index("dp")
    y, x, core = me // 4, (me // 2) % 2, me % 2
    place = jnp.stack([y, x, core, layer == last]).astype(jnp.int32)

    hold = lax.optimization_barrier
    parts = [slice(0, 64), slice(64, 320), slice(320, 384)]

    cuts = [slice(0, 136), slice(136, 280), slice(280, 384)]
    bias_rows = jnp.pad(offsets, ((0, 7), (0, D - BLOCK)))
    w = jnp.concatenate([w, bias_rows], axis=0)
    w_x = x_swap(w)
    w_up, w_down = y_shift(w, 1), y_shift(w, -1)
    p_other = core_swap(p)
    q_mine, q_theirs = split_parity(place, after(q, w))
    q_other = core_swap(q_theirs)
    ahead = [u[t] - q[t] for t in cuts]
    w_x, w_up, w_down, p_other, q_mine, q_other, ahead = hold((w_x, w_up, w_down, p_other, q_mine, q_other, ahead))
    both = jnp.concatenate([p, p_other], axis=0)
    p_top = lax.reduce_precision(both, exponent_bits=8, mantissa_bits=7)
    ph, plo = p_top.astype(jnp.bfloat16), (both - p_top).astype(jnp.bfloat16)
    qs = jnp.concatenate([q_mine, q_other], axis=1)
    w_far, wx_down = y_shift(w_up, 1), y_shift(w_x, -1)
    s0 = depth_shift(ahead[0], 1)
    blocks = [(w, (0, 0)), (w_x, (0, 1))]
    pulled, a_own, (g_own, g_own_x) = layer_step(blocks, ph, plo, qs, None)
    w_far, wx_down, s0, ph, plo, qs, pulled, a_own, g_own, g_own_x = hold(
        (w_far, wx_down, s0, ph, plo, qs, pulled, a_own, g_own, g_own_x)
    )
    wx_up, wx_far = y_shift(w_x, 1), y_shift(wx_down, -1)
    s1 = depth_shift(after(ahead[1], s0), 1)
    blocks = [(w_up, (3, 0)), (w_down, (1, 0)), (w_far, (2, 0)), (wx_down, (1, 1))]
    pulled, a_some, (g_lo, g_hi, g_far, g_hi_x) = layer_step(blocks, ph, plo, qs, pulled)
    wx_up, wx_far, s1, a_some, pulled, g_lo, g_hi, g_far, g_hi_x = hold(
        (wx_up, wx_far, s1, a_some, pulled, g_lo, g_hi, g_far, g_hi_x)
    )
    s2 = depth_shift(after(ahead[2], s1), 1)
    up_x, down = y_shift(g_hi_x, 1), y_shift(g_lo, -1)
    blocks = [(wx_up, (3, 1)), (wx_far, (2, 1))]
    theirs, ours, a_rest, mh, ml, sums = early_step(blocks, ph, plo, qs, pulled)
    theirs, ours, a_rest, mh, s2 = hold((theirs, ours, a_rest, mh, s2))
    pulled_other = core_swap(theirs)
    g_lo_x, g_far_x = late_step(2, ph, plo, mh, ml, sums)
    ours, pulled_other, g_lo_x, g_far_x, a_own, a_some, a_rest = hold(
        (ours, pulled_other, g_lo_x, g_far_x, a_own, a_some, a_rest)
    )
    r = [p[t] - TAU_P * (scaling * (ours[t] + pulled_other[t]) + p[t]) for t in parts]
    r0, r1 = depth_shift(r[0], -1), depth_shift(r[1], -1)
    columns = [
        (a_own[:, :BLOCK], a_own[:, BLOCK:]),
        (a_some[:, BLOCK : 2 * BLOCK], a_some[:, 3 * BLOCK :]),
        (a_some[:, 2 * BLOCK : 3 * BLOCK], a_rest[:, BLOCK:]),
        (a_some[:, :BLOCK], a_rest[:, :BLOCK]),
    ]
    affine = jnp.stack([jnp.concatenate(pair, axis=1) for pair in columns])
    some, rest = affine[:3, rows:], affine[3:, rows:]
    affine_other = (core_swap(some), core_swap(after(rest, up_x, down)))
    r0, up_x, down, affine_mine, affine_other, r_tail = hold(
        (r0, up_x, down, affine[:, :rows], affine_other, r[2])
    )
    args = (place, affine_mine, jnp.concatenate(affine_other, axis=0))
    out = last_step(parts[0], *args, r0, q, u, None)
    far_below, far_above = y_shift(after(g_far, r0), 1), y_shift(after(g_far_x, r0), -1)
    up, down_x = y_shift(g_hi + far_below, 1), y_shift(g_lo_x + far_above, -1)
    own_sum = g_own + down
    x_sum = g_own_x + up_x
    r1, out, own_sum, x_sum, up, down_x = hold((r1, out, own_sum, x_sum, up, down_x))
    from_x = x_swap(x_sum + down_x)
    r2 = depth_shift(r_tail, -1)
    out = last_step(parts[1], *args, r1, q, u, out)
    own_sum = own_sum + up
    moved = jnp.concatenate(r, axis=0) - TAU_P * jnp.concatenate([s0, s1, s2], axis=0)
    inputs_new = jnp.where(layer == 0, p, moved)
    scale_weight = step_weight * scaling
    bias = slice(BLOCK, BLOCK + 1)
    weights_new = weights[0] - scale_weight * own_sum[:BLOCK]
    offsets_new = offsets - step_offset * own_sum[bias, :BLOCK]
    weights_new, offsets_new, inputs_new, out, r2 = hold((weights_new, offsets_new, inputs_new, out, r2))
    outputs_new, mults_new = last_step(parts[2], *args, r2, q, u, out)
    weights_new = weights_new - scale_weight * from_x[:BLOCK]
    offsets_new = offsets_new - step_offset * from_x[bias, :BLOCK]
    return (inputs_new[None], weights_new[None], offsets_new, outputs_new[None], mults_new[None])


def solution(mesh):
    three, two = P("depth", "dp", None), P("depth", "dp")
    specs = (three, three, two, three, three)
    return jax.shard_map(body, mesh=mesh, in_specs=specs, out_specs=specs, check_vma=False)
```

time: 293 us -> 263 us (0.90)
  waiting for transfers between devices: 122 us -> 91.3 us
  starting transfers between devices: 45.9 us -> 36.6 us
  local copies, waits for them, and re-layouts: 7.27 us -> 16.4 us
    ppermute x6, waiting for transfers between devices: 88.1 us -> 44.6 us  [depth_shift(): lax.ppermute(v, 'depth', [(i, i + k) for i in range(n) if 0 <= i + k < n])]
    ppermute x22 -> x19, waiting for transfers between devices: 33.9 us -> 46.7 us  [dp_move(): return lax.ppermute(v, 'dp', [(i, step(i)) for i in range(16)])]
    unnamed x65 -> x80, local copies, waits for them, and re-layouts: 4.11 us -> 15.1 us
    ppermute x22 -> x19, starting transfers between devices: 27.2 us -> 19.3 us  [dp_move(): return lax.ppermute(v, 'dp', [(i, step(i)) for i in range(16)])]
    pallas_call x6 -> x7, Pallas kernels: 78.5 us -> 76 us  [the longest x4 62.4 us: in_tiles(): pl.pallas_call(kernel, grid=(tiles,), out_shape=tuple(out_shape), in_spec...]
    sub x4 -> x6, other arithmetic: 6.23 us -> 7.33 us  [the longest x3 6.01 us: body(): ahead = [u[t] - q[t] for t in cuts]]
  transfers between devices with their start and end apart: 28 -> 25, of which waited for: 9 -> 11; matrix products, arithmetic and copies ran while one was open for 10% -> 11% of each run, Pallas kernels for 20% -> 31%
where the time goes in v2:
time: 263 us; the launch traced here: 259 us
  waiting for transfers between devices  91.3 us (35%)
  Pallas kernels  81 us (31%)
  starting transfers between devices  36.6 us (14%)
  other arithmetic  33 us (13%)
  local copies, waits for them, and re-layouts  16.4 us (6%)
    pallas_call x4, Pallas kernels, in_tiles(): pl.pallas_call(kernel, grid=(tiles,), out_shape=tuple(out_shape), in_spec...  62.4 us
    ppermute x19, waiting for transfers between devices, dp_move(): return lax.ppermute(v, 'dp', [(i, step(i)) for i in range(16)])  46.7 us
    ppermute x6, waiting for transfers between devices, depth_shift(): lax.ppermute(v, 'depth', [(i, i + k) for i in range(n) if 0 <= i + k < n])  44.6 us
    ppermute x19, starting transfers between devices, dp_move(): return lax.ppermute(v, 'dp', [(i, step(i)) for i in range(16)])  19.3 us
    ppermute x6, starting transfers between devices, depth_shift(): lax.ppermute(v, 'depth', [(i, i + k) for i in range(n) if 0 <= i + k < n])  17.3 us
    unnamed x80, local copies, waits for them, and re-layouts  15.1 us
    pallas_call x3, Pallas kernels, last_step(): pl.pallas_call(last_kernel, out_shape=(out, out), grid_spec=pltpu.Prefetc...  13.6 us
    convert_element_type x1, other arithmetic, body(): ph, plo = (p_top.astype(jnp.bfloat16), (both - p_top).astype(jnp.bfloat16))  7.1 us
  transfers between devices with their start and end apart: 25, of which 11 were waited for; matrix products, arithmetic and copies ran while one was open for 11% of the time, Pallas kernels for 31%

profile of v2, /device:TPU:0, one launch (start us, length us, event | category | flops | bytes accessed | tf_op | source)
XLA Modules:
  0.0 259.4 jit_solution(11504972922214028154)
XLA Ops:
  7.6 4.9 %parity.1 = (f32[4,384,256]{2,1,0:T(8,128)}, f32[4,384,256]{2,1,0:T(8,128)}) custom-call(s32[4]{0:T(128)} %pad_add_fusion.s_ref, f32[384,2048]{1,0:T(8,128)} %bitcast.51), custom_call_target="tpu_custom_call" | custom-call | flops 1024 | bytes 1024 | tf_op jit(solution)/shard_map/parity/pallas_call | solution.py:61
  12.6 2.4 subtract_bitcast_fusion.2
  18.6 10.5 %collective-permute-done.refs_1_ = f32[136,2048]{1,0:T(8,128)S(1)} collective-permute-done((f32[136,2048]{1,0:T(8,128)S(1)}, f32[136,2048]{1,0:T(8,128)S(1)}, u32[]{:S(2)}, u32[]{:S(2)}) %collective-permute-start) | collective-permute-done | bytes 1114144 | tf_op jit(solution)/shard_map/ppermute | solution.py:23
  29.1 2.6 collective-permute-done.1.refs_0_
  35.1 4.7 %collective-permute-start.7 = (f32[136,2048]{1,0:T(8,128)S(1)}, f32[136,2048]{1,0:T(8,128)S(1)}, u32[]{:S(2)}, u32[]{:S(2)}) collective-permute-start(f32[136,2048]{1,0:T(8,128)S(1)} %subtract_bitcast_fusion.1), channel_id=1, source_target_pairs={{0,16},{16,32},{32,48},{48,64},{64,80},{80,96},{96,112},{1,17},{17... | collective-permute-start | bytes 3342344 | tf_op jit(solution)/shard_map/ppermute | solution.py:40
  41.8 7.1 %fusion = (bf16[768,2048]{1,0:T(8,128)(2,1)}, bf16[768,2048]{1,0:T(8,128)(2,1)}) fusion(f32[384,2048]{1,0:T(8,128)} %collective-permute-done.3, f32[384,2048]{1,0:T(8,128)S(1)} %bitcast.59), kind=kLoop, calls=%fused_computation.2 | loop fusion | flops 7864320 | bytes 12582912 | tf_op jit(solution)/shard_map/convert_element_type | solution.py:365
  48.9 14.1 %layer_step.2 = (f32[768,2048]{1,0:T(8,128)}, f32[768,256]{1,0:T(8,128)S(1)}, f32[136,2048]{1,0:T(8,128)S(1)}, f32[136,2048]{1,0:T(8,128)S(1)}) custom-call(bf16[768,2048]{1,0:T(8,128)(2,1)} %get-tuple-element.110.ph_ref, bf16[768,2048]{1,0:T(8,128)(2,1)} %get-tuple-element.111.pl_ref, f32[136,2048]{1,0:T(8,128)S(1)} %select_maximum_fusion.refs_0_, ...), custom_call_target="tpu_custom_call" | custom-call | flops 1024 | bytes 1024 | tf_op jit(solution)/shard_map/layer_step/pallas_call | solution.py:247
  65.1 4.1 %collective-permute-start.10 = (f32[144,2048]{1,0:T(8,128)S(1)}, f32[144,2048]{1,0:T(8,128)S(1)}, u32[]{:S(2)}, u32[]{:S(2)}) collective-permute-start(f32[144,2048]{1,0:T(8,128)S(1)} %subtract_bitcast_fusion), channel_id=1, source_target_pairs={{0,16},{16,32},{32,48},{48,64},{64,80},{80,96},{96,112},{1,17},{17... | collective-permute-start | bytes 3538952 | tf_op jit(solution)/shard_map/ppermute | solution.py:40
  69.6 2.9 %collective-permute-start.9 = (f32[136,2048]{1,0:T(8,128)}, f32[136,2048]{1,0:T(8,128)}, u32[]{:S(2)}, u32[]{:S(2)}) collective-permute-start(f32[136,2048]{1,0:T(8,128)} %collective-permute-done.6.refs_3_), channel_id=1, source_target_pairs={{0,12},{1,13},{2,14},{3,15},{4,0},{5,1},{6,2},{7,3},{8,4},{9,5},{1... | collective-permute-start | bytes 3342344 | tf_op jit(solution)/shard_map/ppermute | solution.py:23
  72.5 27.4 %layer_step.3 = (f32[768,2048]{1,0:T(8,128)}, f32[768,512]{1,0:T(8,128)}, f32[136,2048]{1,0:T(8,128)}, f32[136,2048]{1,0:T(8,128)}, f32[136,2048]{1,0:T(8,128)}, /*index=5*/f32[136,2048]{1,0:T(8,128)}) custom-call(bf16[768,2048]{1,0:T(8,128)(2,1)} %get-tuple-element.110.ph_ref, ...), custom_call_target="tpu_custom_call", output_to_operand_aliasing={{0}: (10, {})} | custom-call | flops 1024 | bytes 1024 | tf_op jit(solution)/shard_map/layer_step/pallas_call | solution.py:247
  101.1 4.6 %collective-permute-start.11 = (f32[104,2048]{1,0:T(8,128)}, f32[104,2048]{1,0:T(8,128)S(1)}, u32[]{:S(2)}, u32[]{:S(2)}) collective-permute-start(f32[104,2048]{1,0:T(8,128)} %subtract_bitcast_fusion.2), channel_id=1, source_target_pairs={{0,16},{16,32},{32,48},{48,64},{64,80},{80,96},{96,112},{1,17},{17... | collective-permute-start | bytes 2555912 | tf_op jit(solution)/shard_map/ppermute | solution.py:40
  105.7 15.8 %early_step.1 = (f32[384,2048]{1,0:T(8,128)}, f32[384,2048]{1,0:T(8,128)}, f32[768,256]{1,0:T(8,128)}, bf16[768,256]{1,0:T(8,128)(2,1)}, bf16[768,256]{1,0:T(8,128)(2,1)}, /*index=5*/f32[1,256]{1,0:T(1,128)}) custom-call(bf16[768,2048]{1,0:T(8,128)(2,1)} %get-tuple-element.110.ph_ref, bf16[768,2048]{1,0:T(8,128)(2,1)} %get-tuple-element.111.pl_ref, ...), custom_call_target="tpu_custom_call" | custom-call | flops 1024 | bytes 1024 | tf_op jit(solution)/shard_map/early_step/pallas_call | solution.py:247
  122.0 3.2 %collective-permute-start.16 = (f32[136,2048]{1,0:T(8,128)}, f32[136,2048]{1,0:T(8,128)S(1)}, u32[]{:S(2)}, u32[]{:S(2)}) collective-permute-start(f32[136,2048]{1,0:T(8,128)} %get-tuple-element.149), channel_id=1, source_target_pairs={{0,12},{1,13},{2,14},{3,15},{4,0},{5,1},{6,2},{7,3},{8,4},{9,5},{1... | collective-permute-start | bytes 3342344 | tf_op jit(solution)/shard_map/ppermute | solution.py:23
  129.8 5.0 %late_step.1 = (f32[136,2048]{1,0:T(8,128)S(1)}, f32[136,2048]{1,0:T(8,128)S(1)}) custom-call(bf16[768,2048]{1,0:T(8,128)(2,1)S(1)} %copy-done.1, bf16[768,2048]{1,0:T(8,128)(2,1)S(1)} %copy-done, bf16[768,256]{1,0:T(8,128)(2,1)S(1)} %copy-done.6, bf16[768,256]{1,0:T(8,128)(2,1)S(1)} %copy-done.7, f32[1,256]{1,0:T(1,128)S(1)} %copy-done.8), custom_call_target="tpu_custom_call" | custom-call | flops 1024 | bytes 1024 | tf_op jit(solution)/shard_map/late_step/pallas_call | solution.py:247
  139.5 10.8 %collective-permute-done.15 = f32[136,2048]{1,0:T(8,128)S(1)} collective-permute-done((f32[136,2048]{1,0:T(8,128)}, f32[136,2048]{1,0:T(8,128)S(1)}, u32[]{:S(2)}, u32[]{:S(2)}) %collective-permute-start.15) | collective-permute-done | bytes 1114144 | tf_op jit(solution)/shard_map/ppermute | solution.py:23
  152.2 3.8 %collective-permute-done.14.r_ref = f32[64,2048]{1,0:T(8,128)S(1)} collective-permute-done((f32[64,2048]{1,0:T(8,128)S(1)}, f32[64,2048]{1,0:T(8,128)S(1)}, u32[]{:S(2)}, u32[]{:S(2)}) %collective-permute-start.14) | collective-permute-done | bytes 524320 | tf_op jit(solution)/shard_map/ppermute | solution.py:40
  161.4 20.5 %collective-permute-done.21 = f32[136,2048]{1,0:T(8,128)S(1)} collective-permute-done((f32[136,2048]{1,0:T(8,128)S(1)}, f32[136,2048]{1,0:T(8,128)S(1)}, u32[]{:S(2)}, u32[]{:S(2)}) %collective-permute-start.21) | collective-permute-done | bytes 1114144 | tf_op jit(solution)/shard_map/ppermute | solution.py:23
  188.5 3.5 %last_step.3 = (f32[384,2048]{1,0:T(8,128)}, f32[384,2048]{1,0:T(8,128)}) custom-call(s32[4]{0:T(128)} %pad_add_fusion.s_ref, f32[4,384,256]{2,1,0:T(8,128)} %pad_maximum_fusion.1.mine_ref, f32[4,384,256]{2,1,0:T(8,128)} %copy-done.13, f32[64,2048]{1,0:T(8,128)} %copy-done.34, f32[384,2048]{1,0:T(8,128)} %bitcast.52, f32[384,2048]{1,0:T(8,128)} %bitcast.55), custom_call_target="tpu_custom_call" | custom-call | flops 1024 | bytes 1024 | tf_op jit(solution)/shard_map/last_step/pallas_call | solution.py:104
  194.1 16.7 %collective-permute-done.13.r_ref = f32[256,2048]{1,0:T(8,128)} collective-permute-done((f32[256,2048]{1,0:T(8,128)}, f32[256,2048]{1,0:T(8,128)}, u32[]{:S(2)}, u32[]{:S(2)}) %collective-permute-start.13) | collective-permute-done | bytes 2097184 | tf_op jit(solution)/shard_map/ppermute | solution.py:40
  214.9 3.4 %fusion.1 = f32[384,2048]{1,0:T(8,128)} fusion(f32[64,2048]{1,0:T(8,128)S(1)} %get-tuple-element.178, f32[256,2048]{1,0:T(8,128)} %bitcast_subtract_fusion, f32[64,2048]{1,0:T(8,128)S(1)} %copy-done.17, f32[104,2048]{1,0:T(8,128)S(1)} %copy-done.32, f32[144,2048]{1,0:T(8,128)S(1)} %copy-done.21, f32[136,2048]{1,0:T(8,128)S(1)} %copy-done.23, pred[]{:T(512)S(6)} %eq.10, ...), kind=kLoop, calls=%fused_computation.5 | loop fusion | flops 5505024 | bytes 12582913 | tf_op jit(solution)/shard_map/jit(_where)/select_n | solution.py:417
  219.6 6.7 %last_step.4 = (f32[384,2048]{1,0:T(8,128)}, f32[384,2048]{1,0:T(8,128)}) custom-call(s32[4]{0:T(128)} %pad_add_fusion.s_ref, f32[4,384,256]{2,1,0:T(8,128)} %pad_maximum_fusion.1.mine_ref, f32[4,384,256]{2,1,0:T(8,128)} %copy-done.13, f32[256,2048]{1,0:T(8,128)} %collective-permute-done.13.r_ref, ...), custom_call_target="tpu_custom_call", output_to_operand_aliasing={{0}: (6, {}), {1}: (7, {})} | custom-call | flops 1024 | bytes 1024 | tf_op jit(solution)/shard_map/last_step/pallas_call | solution.py:104
  228.0 23.7 %collective-permute-done.23.r_ref = f32[64,2048]{1,0:T(8,128)S(1)} collective-permute-done((f32[64,2048]{1,0:T(8,128)S(1)}, f32[64,2048]{1,0:T(8,128)S(1)}, u32[]{:S(2)}, u32[]{:S(2)}) %collective-permute-start.23) | collective-permute-done | bytes 524320 | tf_op jit(solution)/shard_map/ppermute | solution.py:40
  252.5 3.4 %last_step.5 = (f32[384,2048]{1,0:T(8,128)}, f32[384,2048]{1,0:T(8,128)}) custom-call(s32[4]{0:T(128)} %pad_add_fusion.s_ref, f32[4,384,256]{2,1,0:T(8,128)} %pad_maximum_fusion.1.mine_ref, f32[4,384,256]{2,1,0:T(8,128)} %copy-done.13, f32[64,2048]{1,0:T(8,128)} %copy-done.35, f32[384,2048]{1,0:T(8,128)} %bitcast.54, ...), custom_call_target="tpu_custom_call", output_to_operand_aliasing={{0}: (6, {}), {1}: (7, {})} | custom-call | flops 1024 | bytes 1024 | tf_op jit(solution)/shard_map/last_step/pallas_call | solution.py:104
  257.1 2.3 fusion.4
  (142 shorter events, 54.1 us)
Async XLA Ops:
  0.6 31.2 %collective-permute-start.3 = (f32[384,2048]{1,0:T(8,128)}, f32[384,2048]{1,0:T(8,128)}, u32[]{:S(2)}, u32[]{:S(2)}) collective-permute-start(f32[384,2048]{1,0:T(8,128)} %bitcast.58), channel_id=1, source_target_pairs={{0,1},{1,0},{2,3},{3,2},{4,5},{5,4},{6,7},{7,6},{8,9},{9,8},{10,11... | collective-permute-start | bytes 9437192 | tf_op jit(solution)/shard_map/ppermute | solution.py:23
  2.1 27.0 %collective-permute-start = (f32[136,2048]{1,0:T(8,128)S(1)}, f32[136,2048]{1,0:T(8,128)S(1)}, u32[]{:S(2)}, u32[]{:S(2)}) collective-permute-start(f32[136,2048]{1,0:T(8,128)S(1)} %select_maximum_fusion.refs_0_), channel_id=1, source_target_pairs={{0,2},{1,3},{2,0},{3,1},{4,6},{5,7},{6,4},{7,5},{8,10},{9,11},{10,... | collective-permute-start | bytes 3342344 | tf_op jit(solution)/shard_map/ppermute | solution.py:23
  3.7 27.9 %collective-permute-start.1 = (f32[136,2048]{1,0:T(8,128)S(1)}, f32[136,2048]{1,0:T(8,128)S(1)}, u32[]{:S(2)}, u32[]{:S(2)}) collective-permute-start(f32[136,2048]{1,0:T(8,128)S(1)} %select_maximum_fusion.refs_0_), channel_id=1, source_target_pairs={{0,4},{1,5},{2,6},{3,7},{4,8},{5,9},{6,10},{7,11},{8,12},{9,13},{1... | collective-permute-start | bytes 3342344 | tf_op jit(solution)/shard_map/ppermute | solution.py:23
  5.3 26.5 %collective-permute-start.2 = (f32[136,2048]{1,0:T(8,128)S(1)}, f32[136,2048]{1,0:T(8,128)}, u32[]{:S(2)}, u32[]{:S(2)}) collective-permute-start(f32[136,2048]{1,0:T(8,128)S(1)} %select_maximum_fusion.refs_0_), channel_id=1, source_target_pairs={{0,12},{1,13},{2,14},{3,15},{4,0},{5,1},{6,2},{7,3},{8,4},{9,5},{1... | collective-permute-start | bytes 3342344 | tf_op jit(solution)/shard_map/ppermute | solution.py:23
  12.6 19.3 %collective-permute-start.4 = (f32[4,384,256]{2,1,0:T(8,128)}, f32[4,384,256]{2,1,0:T(8,128)S(1)}, u32[]{:S(2)}, u32[]{:S(2)}) collective-permute-start(f32[4,384,256]{2,1,0:T(8,128)} %get-tuple-element.99), channel_id=1, source_target_pairs={{0,1},{1,0},{2,3},{3,2},{4,5},{5,4},{6,7},{7,6},{8,9},{9,8},{10,11... | collective-permute-start | bytes 4718600 | tf_op jit(solution)/shard_map/ppermute | solution.py:23
  31.8 33.2 %collective-permute-start.5 = (f32[136,2048]{1,0:T(8,128)S(1)}, f32[136,2048]{1,0:T(8,128)S(1)}, u32[]{:S(2)}, u32[]{:S(2)}) collective-permute-start(f32[136,2048]{1,0:T(8,128)S(1)} %collective-permute-done.1.refs_0_), channel_id=1, source_target_pairs={{0,4},{1,5},{2,6},{3,7},{4,8},{5,9},{6,10},{7,11},{8,12},{9,13},{1... | collective-permute-start | bytes 3342344 | tf_op jit(solution)/shard_map/ppermute | solution.py:23
  33.4 31.6 %collective-permute-start.6 = (f32[136,2048]{1,0:T(8,128)S(1)}, f32[136,2048]{1,0:T(8,128)}, u32[]{:S(2)}, u32[]{:S(2)}) collective-permute-start(f32[136,2048]{1,0:T(8,128)S(1)} %collective-permute-done.refs_1_), channel_id=1, source_target_pairs={{0,12},{1,13},{2,14},{3,15},{4,0},{5,1},{6,2},{7,3},{8,4},{9,5},{1... | collective-permute-start | bytes 3342344 | tf_op jit(solution)/shard_map/ppermute | solution.py:23
  35.1 30.0 %collective-permute-start.7 = (f32[136,2048]{1,0:T(8,128)S(1)}, f32[136,2048]{1,0:T(8,128)S(1)}, u32[]{:S(2)}, u32[]{:S(2)}) collective-permute-start(f32[136,2048]{1,0:T(8,128)S(1)} %subtract_bitcast_fusion.1), channel_id=1, source_target_pairs={{0,16},{16,32},{32,48},{48,64},{64,80},{80,96},{96,112},{1,17},{17... | collective-permute-start | bytes 3342344 | tf_op jit(solution)/shard_map/ppermute | solution.py:40
  65.1 34.9 %collective-permute-start.10 = (f32[144,2048]{1,0:T(8,128)S(1)}, f32[144,2048]{1,0:T(8,128)S(1)}, u32[]{:S(2)}, u32[]{:S(2)}) collective-permute-start(f32[144,2048]{1,0:T(8,128)S(1)} %subtract_bitcast_fusion), channel_id=1, source_target_pairs={{0,16},{16,32},{32,48},{48,64},{64,80},{80,96},{96,112},{1,17},{17... | collective-permute-start | bytes 3538952 | tf_op jit(solution)/shard_map/ppermute | solution.py:40
  69.2 30.8 %collective-permute-start.8 = (f32[136,2048]{1,0:T(8,128)S(1)}, f32[136,2048]{1,0:T(8,128)S(1)}, u32[]{:S(2)}, u32[]{:S(2)}) collective-permute-start(f32[136,2048]{1,0:T(8,128)S(1)} %collective-permute-done.refs_1_), channel_id=1, source_target_pairs={{0,4},{1,5},{2,6},{3,7},{4,8},{5,9},{6,10},{7,11},{8,12},{9,13},{1... | collective-permute-start | bytes 3342344 | tf_op jit(solution)/shard_map/ppermute | solution.py:23
  69.6 30.4 %collective-permute-start.9 = (f32[136,2048]{1,0:T(8,128)}, f32[136,2048]{1,0:T(8,128)}, u32[]{:S(2)}, u32[]{:S(2)}) collective-permute-start(f32[136,2048]{1,0:T(8,128)} %collective-permute-done.6.refs_3_), channel_id=1, source_target_pairs={{0,12},{1,13},{2,14},{3,15},{4,0},{5,1},{6,2},{7,3},{8,4},{9,5},{1... | collective-permute-start | bytes 3342344 | tf_op jit(solution)/shard_map/ppermute | solution.py:23
  101.1 20.9 %collective-permute-start.11 = (f32[104,2048]{1,0:T(8,128)}, f32[104,2048]{1,0:T(8,128)S(1)}, u32[]{:S(2)}, u32[]{:S(2)}) collective-permute-start(f32[104,2048]{1,0:T(8,128)} %subtract_bitcast_fusion.2), channel_id=1, source_target_pairs={{0,16},{16,32},{32,48},{48,64},{64,80},{80,96},{96,112},{1,17},{17... | collective-permute-start | bytes 2555912 | tf_op jit(solution)/shard_map/ppermute | solution.py:40
  122.0 12.9 %collective-permute-start.12 = (f32[384,2048]{1,0:T(8,128)}, f32[384,2048]{1,0:T(8,128)S(1)}, u32[]{:S(2)}, u32[]{:S(2)}) collective-permute-start(f32[384,2048]{1,0:T(8,128)} %get-tuple-element.137), channel_id=1, source_target_pairs={{0,1},{1,0},{2,3},{3,2},{4,5},{5,4},{6,7},{7,6},{8,9},{9,8},{10,11... | collective-permute-start | bytes 9437192 | tf_op jit(solution)/shard_map/ppermute | solution.py:23
  122.0 28.4 %collective-permute-start.15 = (f32[136,2048]{1,0:T(8,128)}, f32[136,2048]{1,0:T(8,128)S(1)}, u32[]{:S(2)}, u32[]{:S(2)}) collective-permute-start(f32[136,2048]{1,0:T(8,128)} %get-tuple-element.148), channel_id=1, source_target_pairs={{0,4},{1,5},{2,6},{3,7},{4,8},{5,9},{6,10},{7,11},{8,12},{9,13},{1... | collective-permute-start | bytes 3342344 | tf_op jit(solution)/shard_map/ppermute | solution.py:23
  122.0 28.4 %collective-permute-start.16 = (f32[136,2048]{1,0:T(8,128)}, f32[136,2048]{1,0:T(8,128)S(1)}, u32[]{:S(2)}, u32[]{:S(2)}) collective-permute-start(f32[136,2048]{1,0:T(8,128)} %get-tuple-element.149), channel_id=1, source_target_pairs={{0,12},{1,13},{2,14},{3,15},{4,0},{5,1},{6,2},{7,3},{8,4},{9,5},{1... | collective-permute-start | bytes 3342344 | tf_op jit(solution)/shard_map/ppermute | solution.py:23
  135.3 20.7 %collective-permute-start.17 = (f32[3,384,256]{2,1,0:T(8,128)S(1)}, f32[3,384,256]{2,1,0:T(8,128)S(1)}, u32[]{:S(2)}, u32[]{:S(2)}) collective-permute-start(f32[3,384,256]{2,1,0:T(8,128)S(1)} %pad_maximum_fusion.4), channel_id=1, source_target_pairs={{0,1},{1,0},{2,3},{3,2},{4,5},{5,4},{6,7},{7,6},{8,9},{9,8},{10,11... | collective-permute-start | bytes 3538952 | tf_op jit(solution)/shard_map/ppermute | solution.py:23
  138.1 17.8 %collective-permute-start.14 = (f32[64,2048]{1,0:T(8,128)S(1)}, f32[64,2048]{1,0:T(8,128)S(1)}, u32[]{:S(2)}, u32[]{:S(2)}) collective-permute-start(f32[64,2048]{1,0:T(8,128)S(1)} %get-tuple-element.190), channel_id=1, source_target_pairs={{16,0},{32,16},{48,32},{64,48},{80,64},{96,80},{112,96},{17,1},{33... | collective-permute-start | bytes 1572872 | tf_op jit(solution)/shard_map/ppermute | solution.py:40
  156.0 25.9 %collective-permute-start.21 = (f32[136,2048]{1,0:T(8,128)S(1)}, f32[136,2048]{1,0:T(8,128)S(1)}, u32[]{:S(2)}, u32[]{:S(2)}) collective-permute-start(f32[136,2048]{1,0:T(8,128)S(1)} %get-tuple-element.169), channel_id=1, source_target_pairs={{0,12},{1,13},{2,14},{3,15},{4,0},{5,1},{6,2},{7,3},{8,4},{9,5},{1... | collective-permute-start | bytes 3342344 | tf_op jit(solution)/shard_map/ppermute | solution.py:23
  156.3 28.6 %collective-permute-start.19 = (f32[136,2048]{1,0:T(8,128)S(1)}, f32[136,2048]{1,0:T(8,128)S(1)}, u32[]{:S(2)}, u32[]{:S(2)}) collective-permute-start(f32[136,2048]{1,0:T(8,128)S(1)} %copy-done.38), channel_id=1, source_target_pairs={{0,4},{1,5},{2,6},{3,7},{4,8},{5,9},{6,10},{7,11},{8,12},{9,13},{1... | collective-permute-start | bytes 3342344 | tf_op jit(solution)/shard_map/ppermute | solution.py:23
  160.0 50.8 %collective-permute-start.13 = (f32[256,2048]{1,0:T(8,128)}, f32[256,2048]{1,0:T(8,128)}, u32[]{:S(2)}, u32[]{:S(2)}) collective-permute-start(f32[256,2048]{1,0:T(8,128)} %bitcast_subtract_fusion), channel_id=1, source_target_pairs={{16,0},{32,16},{48,32},{64,48},{80,64},{96,80},{112,96},{17,1},{33... | collective-permute-start | bytes 6291464 | tf_op jit(solution)/shard_map/ppermute | solution.py:40
  183.1 27.8 %collective-permute-start.22 = (f32[136,2048]{1,0:T(8,128)}, f32[136,2048]{1,0:T(8,128)}, u32[]{:S(2)}, u32[]{:S(2)}) collective-permute-start(f32[136,2048]{1,0:T(8,128)} %add.58), channel_id=1, source_target_pairs={{0,12},{1,13},{2,14},{3,15},{4,0},{5,1},{6,2},{7,3},{8,4},{9,5},{1... | collective-permute-start | bytes 3342344 | tf_op jit(solution)/shard_map/ppermute | solution.py:23
  186.0 26.7 %collective-permute-start.20 = (f32[136,2048]{1,0:T(8,128)}, f32[136,2048]{1,0:T(8,128)}, u32[]{:S(2)}, u32[]{:S(2)}) collective-permute-start(f32[136,2048]{1,0:T(8,128)} %add.57), channel_id=1, source_target_pairs={{0,4},{1,5},{2,6},{3,7},{4,8},{5,9},{6,10},{7,11},{8,12},{9,13},{1... | collective-permute-start | bytes 3342344 | tf_op jit(solution)/shard_map/ppermute | solution.py:23
  214.3 41.7 %collective-permute-start.24 = (f32[136,2048]{1,0:T(8,128)S(1)}, f32[136,2048]{1,0:T(8,128)}, u32[]{:S(2)}, u32[]{:S(2)}) collective-permute-start(f32[136,2048]{1,0:T(8,128)S(1)} %add.60), channel_id=1, source_target_pairs={{0,2},{1,3},{2,0},{3,1},{4,6},{5,7},{6,4},{7,5},{8,10},{9,11},{10,... | collective-permute-start | bytes 3342344 | tf_op jit(solution)/shard_map/ppermute | solution.py:23
  218.4 33.4 %collective-permute-start.23 = (f32[64,2048]{1,0:T(8,128)S(1)}, f32[64,2048]{1,0:T(8,128)S(1)}, u32[]{:S(2)}, u32[]{:S(2)}) collective-permute-start(f32[64,2048]{1,0:T(8,128)S(1)} %get-tuple-element.178), channel_id=1, source_target_pairs={{16,0},{32,16},{48,32},{64,48},{80,64},{96,80},{112,96},{17,1},{33... | collective-permute-start | bytes 1572872 | tf_op jit(solution)/shard_map/ppermute | solution.py:40
  (40 other events, 272.9 us)

commit v3 on v2

--- a/solution.py
+++ b/solution.py
@@ -359,10 +359,10 @@
     q_mine, q_theirs = split_parity(place, after(q, w))
     q_other = core_swap(q_theirs)
     ahead = [u[t] - q[t] for t in cuts]
-    w_x, w_up, w_down, p_other, q_mine, q_other, ahead = hold((w_x, w_up, w_down, p_other, q_mine, q_other, ahead))
     both = jnp.concatenate([p, p_other], axis=0)
     p_top = lax.reduce_precision(both, exponent_bits=8, mantissa_bits=7)
     ph, plo = p_top.astype(jnp.bfloat16), (both - p_top).astype(jnp.bfloat16)
+    w_x, w_up, w_down, ph, plo, q_mine, q_other, ahead = hold((w_x, w_up, w_down, ph, plo, q_mine, q_other, ahead))
     qs = jnp.concatenate([q_mine, q_other], axis=1)
     w_far, wx_down = y_shift(w_up, 1), y_shift(w_x, -1)
     s0 = depth_shift(ahead[0], 1)
@@ -408,13 +408,13 @@
     up, down_x = y_shift(g_hi + far_below, 1), y_shift(g_lo_x + far_above, -1)
     own_sum = g_own + down
     x_sum = g_own_x + up_x
-    r1, out, own_sum, x_sum, up, down_x = hold((r1, out, own_sum, x_sum, up, down_x))
+    moved = jnp.concatenate(r, axis=0) - TAU_P * jnp.concatenate([s0, s1, s2], axis=0)
+    inputs_new = jnp.where(layer == 0, p, moved)
+    r1, out, own_sum, x_sum, up, down_x, inputs_new = hold((r1, out, own_sum, x_sum, up, down_x, inputs_new))
     from_x = x_swap(x_sum + down_x)
     r2 = depth_shift(r_tail, -1)
     out = last_step(parts[1], *args, r1, q, u, out)
     own_sum = own_sum + up
-    moved = jnp.concatenate(r, axis=0) - TAU_P * jnp.concatenate([s0, s1, s2], axis=0)
-    inputs_new = jnp.where(layer == 0, p, moved)
     scale_weight = step_weight * scaling
     bias = slice(BLOCK, BLOCK + 1)
     weights_new = weights[0] - scale_weight * own_sum[:BLOCK]

time: 263 us -> 261 us (level)
  waiting for transfers between devices: 91.3 us -> 88.3 us
    ppermute x19, waiting for transfers between devices: 46.7 us -> 39.9 us  [dp_move(): return lax.ppermute(v, 'dp', [(i, step(i)) for i in range(16)])]
    ppermute x6, waiting for transfers between devices: 44.6 us -> 48.4 us  [depth_shift(): lax.ppermute(v, 'depth', [(i, i + k) for i in range(n) if 0 <= i + k < n])]
    unnamed x80 -> x74, local copies, waits for them, and re-layouts: 15.1 us -> 16.6 us
  transfers between devices with their start and end apart: 25 -> 25, of which waited for: 11 -> 10; matrix products, arithmetic and copies ran while one was open for 11% -> 11% of each run, Pallas kernels for 31% -> 31%
where the time goes in v3:
time: 261 us; the launch traced here: 260 us
  waiting for transfers between devices  88.3 us (34%)
  Pallas kernels  81.1 us (31%)
  starting transfers between devices  39.2 us (15%)
  other arithmetic  33.3 us (13%)
  local copies, waits for them, and re-layouts  16.9 us (6%)
    pallas_call x4, Pallas kernels, in_tiles(): pl.pallas_call(kernel, grid=(tiles,), out_shape=tuple(out_shape), in_spec...  62.5 us
    ppermute x6, waiting for transfers between devices, depth_shift(): lax.ppermute(v, 'depth', [(i, i + k) for i in range(n) if 0 <= i + k < n])  48.4 us
    ppermute x19, waiting for transfers between devices, dp_move(): return lax.ppermute(v, 'dp', [(i, step(i)) for i in range(16)])  39.9 us
    ppermute x19, starting transfers between devices, dp_move(): return lax.ppermute(v, 'dp', [(i, step(i)) for i in range(16)])  19.7 us
    ppermute x6, starting transfers between devices, depth_shift(): lax.ppermute(v, 'depth', [(i, i + k) for i in range(n) if 0 <= i + k < n])  19.5 us
    unnamed x74, local copies, waits for them, and re-layouts  16.6 us
    pallas_call x3, Pallas kernels, last_step(): pl.pallas_call(last_kernel, out_shape=(out, out), grid_spec=pltpu.Prefetc...  13.6 us
    convert_element_type x1, other arithmetic, body(): ph, plo = (p_top.astype(jnp.bfloat16), (both - p_top).astype(jnp.bfloat16))  5.96 us
  transfers between devices with their start and end apart: 25, of which 10 were waited for; matrix products, arithmetic and copies ran while one was open for 11% of the time, Pallas kernels for 31%

profile of v3, /device:TPU:0, one launch (start us, length us, event | category | flops | bytes accessed | tf_op | source)
XLA Modules:
  0.0 259.9 jit_solution(11744117666579217252)
XLA Ops:
  7.6 5.0 %parity.1 = (f32[4,384,256]{2,1,0:T(8,128)}, f32[4,384,256]{2,1,0:T(8,128)}) custom-call(s32[4]{0:T(128)} %pad_add_fusion.s_ref, f32[384,2048]{1,0:T(8,128)} %bitcast.51), custom_call_target="tpu_custom_call" | custom-call | flops 1024 | bytes 1024 | tf_op jit(solution)/shard_map/parity/pallas_call | solution.py:61
  19.6 6.0 %fusion = (bf16[768,2048]{1,0:T(8,128)(2,1)}, bf16[768,2048]{1,0:T(8,128)(2,1)}) fusion(f32[384,2048]{1,0:T(8,128)} %collective-permute-done.3, f32[384,2048]{1,0:T(8,128)S(1)} %bitcast.59), kind=kLoop, calls=%fused_computation.2 | loop fusion | flops 7864320 | bytes 12582912 | tf_op jit(solution)/shard_map/convert_element_type | solution.py:364
  25.5 3.6 %collective-permute-done.refs_1_ = f32[136,2048]{1,0:T(8,128)S(1)} collective-permute-done((f32[136,2048]{1,0:T(8,128)S(1)}, f32[136,2048]{1,0:T(8,128)S(1)}, u32[]{:S(2)}, u32[]{:S(2)}) %collective-permute-start) | collective-permute-done | bytes 1114144 | tf_op jit(solution)/shard_map/ppermute | solution.py:23
  29.1 2.7 %collective-permute-done.1.refs_0_ = f32[136,2048]{1,0:T(8,128)} collective-permute-done((f32[136,2048]{1,0:T(8,128)S(1)}, f32[136,2048]{1,0:T(8,128)}, u32[]{:S(2)}, u32[]{:S(2)}) %collective-permute-start.1) | collective-permute-done | bytes 1114144 | tf_op jit(solution)/shard_map/ppermute | solution.py:23
  35.1 4.7 %collective-permute-start.7 = (f32[136,2048]{1,0:T(8,128)S(1)}, f32[136,2048]{1,0:T(8,128)S(1)}, u32[]{:S(2)}, u32[]{:S(2)}) collective-permute-start(f32[136,2048]{1,0:T(8,128)S(1)} %subtract_bitcast_fusion.1), channel_id=1, source_target_pairs={{0,16},{16,32},{32,48},{48,64},{64,80},{80,96},{96,112},{1,17},{17... | collective-permute-start | bytes 3342344 | tf_op jit(solution)/shard_map/ppermute | solution.py:40
  41.7 14.1 %layer_step.2 = (f32[768,2048]{1,0:T(8,128)}, f32[768,256]{1,0:T(8,128)S(1)}, f32[136,2048]{1,0:T(8,128)S(1)}, f32[136,2048]{1,0:T(8,128)S(1)}) custom-call(bf16[768,2048]{1,0:T(8,128)(2,1)} %get-tuple-element.113.ph_ref, bf16[768,2048]{1,0:T(8,128)(2,1)} %get-tuple-element.114.pl_ref, f32[136,2048]{1,0:T(8,128)S(1)} %select_maximum_fusion.refs_0_, ...), custom_call_target="tpu_custom_call" | custom-call | flops 1024 | bytes 1024 | tf_op jit(solution)/shard_map/layer_step/pallas_call | solution.py:247
  59.2 3.4 %collective-permute-done.7 = f32[136,2048]{1,0:T(8,128)S(1)} collective-permute-done((f32[136,2048]{1,0:T(8,128)S(1)}, f32[136,2048]{1,0:T(8,128)S(1)}, u32[]{:S(2)}, u32[]{:S(2)}) %collective-permute-start.7) | collective-permute-done | bytes 1114144 | tf_op jit(solution)/shard_map/ppermute | solution.py:40
  62.5 6.0 %collective-permute-start.10 = (f32[144,2048]{1,0:T(8,128)S(1)}, f32[144,2048]{1,0:T(8,128)S(1)}, u32[]{:S(2)}, u32[]{:S(2)}) collective-permute-start(f32[144,2048]{1,0:T(8,128)S(1)} %subtract_bitcast_fusion), channel_id=1, source_target_pairs={{0,16},{16,32},{32,48},{48,64},{64,80},{80,96},{96,112},{1,17},{17... | collective-permute-start | bytes 3538952 | tf_op jit(solution)/shard_map/ppermute | solution.py:40
  68.6 3.2 %collective-permute-start.9 = (f32[136,2048]{1,0:T(8,128)}, f32[136,2048]{1,0:T(8,128)}, u32[]{:S(2)}, u32[]{:S(2)}) collective-permute-start(f32[136,2048]{1,0:T(8,128)} %collective-permute-done.6.refs_3_), channel_id=1, source_target_pairs={{0,12},{1,13},{2,14},{3,15},{4,0},{5,1},{6,2},{7,3},{8,4},{9,5},{1... | collective-permute-start | bytes 3342344 | tf_op jit(solution)/shard_map/ppermute | solution.py:23
  71.8 27.5 %layer_step.3 = (f32[768,2048]{1,0:T(8,128)}, f32[768,512]{1,0:T(8,128)}, f32[136,2048]{1,0:T(8,128)}, f32[136,2048]{1,0:T(8,128)}, f32[136,2048]{1,0:T(8,128)}, /*index=5*/f32[136,2048]{1,0:T(8,128)}) custom-call(bf16[768,2048]{1,0:T(8,128)(2,1)} %get-tuple-element.113.ph_ref, ...), custom_call_target="tpu_custom_call", output_to_operand_aliasing={{0}: (10, {})} | custom-call | flops 1024 | bytes 1024 | tf_op jit(solution)/shard_map/layer_step/pallas_call | solution.py:247
  100.9 4.9 %collective-permute-start.11 = (f32[104,2048]{1,0:T(8,128)}, f32[104,2048]{1,0:T(8,128)S(1)}, u32[]{:S(2)}, u32[]{:S(2)}) collective-permute-start(f32[104,2048]{1,0:T(8,128)} %subtract_bitcast_fusion.2), channel_id=1, source_target_pairs={{0,16},{16,32},{32,48},{48,64},{64,80},{80,96},{96,112},{1,17},{17... | collective-permute-start | bytes 2555912 | tf_op jit(solution)/shard_map/ppermute | solution.py:40
  105.8 15.8 %early_step.1 = (f32[384,2048]{1,0:T(8,128)}, f32[384,2048]{1,0:T(8,128)}, f32[768,256]{1,0:T(8,128)}, bf16[768,256]{1,0:T(8,128)(2,1)}, bf16[768,256]{1,0:T(8,128)(2,1)}, /*index=5*/f32[1,256]{1,0:T(1,128)}) custom-call(bf16[768,2048]{1,0:T(8,128)(2,1)} %get-tuple-element.113.ph_ref, bf16[768,2048]{1,0:T(8,128)(2,1)} %get-tuple-element.114.pl_ref, ...), custom_call_target="tpu_custom_call" | custom-call | flops 1024 | bytes 1024 | tf_op jit(solution)/shard_map/early_step/pallas_call | solution.py:247
  121.8 3.2 %collective-permute-start.16 = (f32[136,2048]{1,0:T(8,128)}, f32[136,2048]{1,0:T(8,128)S(1)}, u32[]{:S(2)}, u32[]{:S(2)}) collective-permute-start(f32[136,2048]{1,0:T(8,128)} %get-tuple-element.152), channel_id=1, source_target_pairs={{0,12},{1,13},{2,14},{3,15},{4,0},{5,1},{6,2},{7,3},{8,4},{9,5},{1... | collective-permute-start | bytes 3342344 | tf_op jit(solution)/shard_map/ppermute | solution.py:23
  129.6 5.0 %late_step.1 = (f32[136,2048]{1,0:T(8,128)S(1)}, f32[136,2048]{1,0:T(8,128)S(1)}) custom-call(bf16[768,2048]{1,0:T(8,128)(2,1)S(1)} %copy-done.1, bf16[768,2048]{1,0:T(8,128)(2,1)S(1)} %copy-done, bf16[768,256]{1,0:T(8,128)(2,1)S(1)} %copy-done.6, bf16[768,256]{1,0:T(8,128)(2,1)S(1)} %copy-done.7, f32[1,256]{1,0:T(1,128)S(1)} %copy-done.8), custom_call_target="tpu_custom_call" | custom-call | flops 1024 | bytes 1024 | tf_op jit(solution)/shard_map/late_step/pallas_call | solution.py:247
  140.1 10.0 %collective-permute-done.15 = f32[136,2048]{1,0:T(8,128)S(1)} collective-permute-done((f32[136,2048]{1,0:T(8,128)}, f32[136,2048]{1,0:T(8,128)S(1)}, u32[]{:S(2)}, u32[]{:S(2)}) %collective-permute-start.15) | collective-permute-done | bytes 1114144 | tf_op jit(solution)/shard_map/ppermute | solution.py:23
  152.0 4.2 %collective-permute-done.14.r_ref = f32[64,2048]{1,0:T(8,128)S(1)} collective-permute-done((f32[64,2048]{1,0:T(8,128)S(1)}, f32[64,2048]{1,0:T(8,128)S(1)}, u32[]{:S(2)}, u32[]{:S(2)}) %collective-permute-start.14) | collective-permute-done | bytes 524320 | tf_op jit(solution)/shard_map/ppermute | solution.py:40
  161.8 20.4 %collective-permute-done.21 = f32[136,2048]{1,0:T(8,128)S(1)} collective-permute-done((f32[136,2048]{1,0:T(8,128)S(1)}, f32[136,2048]{1,0:T(8,128)S(1)}, u32[]{:S(2)}, u32[]{:S(2)}) %collective-permute-start.21) | collective-permute-done | bytes 1114144 | tf_op jit(solution)/shard_map/ppermute | solution.py:23
  186.5 4.5 %fusion.1 = f32[384,2048]{1,0:T(8,128)} fusion(f32[64,2048]{1,0:T(8,128)} %get-tuple-element.182, f32[256,2048]{1,0:T(8,128)} %bitcast_subtract_fusion, f32[64,2048]{1,0:T(8,128)} %copy-done.17, f32[104,2048]{1,0:T(8,128)} %copy-done.30, f32[144,2048]{1,0:T(8,128)} %copy-done.20, f32[136,2048]{1,0:T(8,128)} %copy-done.23, pred[]{:T(512)S(6)} %eq.10, ...), kind=kLoop, calls=%fused_computation.5 | loop fusion | flops 5505024 | bytes 12582913 | tf_op jit(solution)/shard_map/jit(_where)/select_n | solution.py:412
  192.3 3.5 %last_step.3 = (f32[384,2048]{1,0:T(8,128)}, f32[384,2048]{1,0:T(8,128)}) custom-call(s32[4]{0:T(128)} %pad_add_fusion.s_ref, f32[4,384,256]{2,1,0:T(8,128)} %pad_maximum_fusion.1.mine_ref, f32[4,384,256]{2,1,0:T(8,128)} %copy-done.13, f32[64,2048]{1,0:T(8,128)} %copy-done.32, f32[384,2048]{1,0:T(8,128)} %bitcast.52, f32[384,2048]{1,0:T(8,128)} %bitcast.55), custom_call_target="tpu_custom_call" | custom-call | flops 1024 | bytes 1024 | tf_op jit(solution)/shard_map/last_step/pallas_call | solution.py:104
  197.9 13.2 %collective-permute-done.13.r_ref = f32[256,2048]{1,0:T(8,128)} collective-permute-done((f32[256,2048]{1,0:T(8,128)}, f32[256,2048]{1,0:T(8,128)}, u32[]{:S(2)}, u32[]{:S(2)}) %collective-permute-start.13) | collective-permute-done | bytes 2097184 | tf_op jit(solution)/shard_map/ppermute | solution.py:40
  216.3 6.7 %last_step.4 = (f32[384,2048]{1,0:T(8,128)}, f32[384,2048]{1,0:T(8,128)}) custom-call(s32[4]{0:T(128)} %pad_add_fusion.s_ref, f32[4,384,256]{2,1,0:T(8,128)} %pad_maximum_fusion.1.mine_ref, f32[4,384,256]{2,1,0:T(8,128)} %copy-done.13, f32[256,2048]{1,0:T(8,128)} %collective-permute-done.13.r_ref, ...), custom_call_target="tpu_custom_call", output_to_operand_aliasing={{0}: (6, {}), {1}: (7, {})} | custom-call | flops 1024 | bytes 1024 | tf_op jit(solution)/shard_map/last_step/pallas_call | solution.py:104
  224.6 27.6 %collective-permute-done.23.r_ref = f32[64,2048]{1,0:T(8,128)S(1)} collective-permute-done((f32[64,2048]{1,0:T(8,128)S(1)}, f32[64,2048]{1,0:T(8,128)S(1)}, u32[]{:S(2)}, u32[]{:S(2)}) %collective-permute-start.23) | collective-permute-done | bytes 524320 | tf_op jit(solution)/shard_map/ppermute | solution.py:40
  253.0 3.4 %last_step.5 = (f32[384,2048]{1,0:T(8,128)}, f32[384,2048]{1,0:T(8,128)}) custom-call(s32[4]{0:T(128)} %pad_add_fusion.s_ref, f32[4,384,256]{2,1,0:T(8,128)} %pad_maximum_fusion.1.mine_ref, f32[4,384,256]{2,1,0:T(8,128)} %copy-done.13, f32[64,2048]{1,0:T(8,128)} %copy-done.33, f32[384,2048]{1,0:T(8,128)} %bitcast.54, ...), custom_call_target="tpu_custom_call", output_to_operand_aliasing={{0}: (6, {}), {1}: (7, {})} | custom-call | flops 1024 | bytes 1024 | tf_op jit(solution)/shard_map/last_step/pallas_call | solution.py:104
  257.6 2.3 fusion.4
  (136 shorter events, 57.8 us)
Async XLA Ops:
  0.6 18.3 %collective-permute-start.3 = (f32[384,2048]{1,0:T(8,128)}, f32[384,2048]{1,0:T(8,128)}, u32[]{:S(2)}, u32[]{:S(2)}) collective-permute-start(f32[384,2048]{1,0:T(8,128)} %bitcast.58), channel_id=1, source_target_pairs={{0,1},{1,0},{2,3},{3,2},{4,5},{5,4},{6,7},{7,6},{8,9},{9,8},{10,11... | collective-permute-start | bytes 9437192 | tf_op jit(solution)/shard_map/ppermute | solution.py:23
  2.1 27.0 %collective-permute-start = (f32[136,2048]{1,0:T(8,128)S(1)}, f32[136,2048]{1,0:T(8,128)S(1)}, u32[]{:S(2)}, u32[]{:S(2)}) collective-permute-start(f32[136,2048]{1,0:T(8,128)S(1)} %select_maximum_fusion.refs_0_), channel_id=1, source_target_pairs={{0,2},{1,3},{2,0},{3,1},{4,6},{5,7},{6,4},{7,5},{8,10},{9,11},{10,... | collective-permute-start | bytes 3342344 | tf_op jit(solution)/shard_map/ppermute | solution.py:23
  3.7 28.1 %collective-permute-start.1 = (f32[136,2048]{1,0:T(8,128)S(1)}, f32[136,2048]{1,0:T(8,128)}, u32[]{:S(2)}, u32[]{:S(2)}) collective-permute-start(f32[136,2048]{1,0:T(8,128)S(1)} %select_maximum_fusion.refs_0_), channel_id=1, source_target_pairs={{0,4},{1,5},{2,6},{3,7},{4,8},{5,9},{6,10},{7,11},{8,12},{9,13},{1... | collective-permute-start | bytes 3342344 | tf_op jit(solution)/shard_map/ppermute | solution.py:23
  5.3 26.5 %collective-permute-start.2 = (f32[136,2048]{1,0:T(8,128)S(1)}, f32[136,2048]{1,0:T(8,128)}, u32[]{:S(2)}, u32[]{:S(2)}) collective-permute-start(f32[136,2048]{1,0:T(8,128)S(1)} %select_maximum_fusion.refs_0_), channel_id=1, source_target_pairs={{0,12},{1,13},{2,14},{3,15},{4,0},{5,1},{6,2},{7,3},{8,4},{9,5},{1... | collective-permute-start | bytes 3342344 | tf_op jit(solution)/shard_map/ppermute | solution.py:23
  12.6 19.2 %collective-permute-start.4 = (f32[4,384,256]{2,1,0:T(8,128)}, f32[4,384,256]{2,1,0:T(8,128)S(1)}, u32[]{:S(2)}, u32[]{:S(2)}) collective-permute-start(f32[4,384,256]{2,1,0:T(8,128)} %get-tuple-element.101), channel_id=1, source_target_pairs={{0,1},{1,0},{2,3},{3,2},{4,5},{5,4},{6,7},{7,6},{8,9},{9,8},{10,11... | collective-permute-start | bytes 4718600 | tf_op jit(solution)/shard_map/ppermute | solution.py:23
  31.8 27.3 %collective-permute-start.5 = (f32[136,2048]{1,0:T(8,128)}, f32[136,2048]{1,0:T(8,128)S(1)}, u32[]{:S(2)}, u32[]{:S(2)}) collective-permute-start(f32[136,2048]{1,0:T(8,128)} %collective-permute-done.1.refs_0_), channel_id=1, source_target_pairs={{0,4},{1,5},{2,6},{3,7},{4,8},{5,9},{6,10},{7,11},{8,12},{9,13},{1... | collective-permute-start | bytes 3342344 | tf_op jit(solution)/shard_map/ppermute | solution.py:23
  33.4 25.8 %collective-permute-start.6 = (f32[136,2048]{1,0:T(8,128)S(1)}, f32[136,2048]{1,0:T(8,128)}, u32[]{:S(2)}, u32[]{:S(2)}) collective-permute-start(f32[136,2048]{1,0:T(8,128)S(1)} %collective-permute-done.refs_1_), channel_id=1, source_target_pairs={{0,12},{1,13},{2,14},{3,15},{4,0},{5,1},{6,2},{7,3},{8,4},{9,5},{1... | collective-permute-start | bytes 3342344 | tf_op jit(solution)/shard_map/ppermute | solution.py:23
  35.1 27.5 %collective-permute-start.7 = (f32[136,2048]{1,0:T(8,128)S(1)}, f32[136,2048]{1,0:T(8,128)S(1)}, u32[]{:S(2)}, u32[]{:S(2)}) collective-permute-start(f32[136,2048]{1,0:T(8,128)S(1)} %subtract_bitcast_fusion.1), channel_id=1, source_target_pairs={{0,16},{16,32},{32,48},{48,64},{64,80},{80,96},{96,112},{1,17},{17... | collective-permute-start | bytes 3342344 | tf_op jit(solution)/shard_map/ppermute | solution.py:40
  62.5 36.8 %collective-permute-start.10 = (f32[144,2048]{1,0:T(8,128)S(1)}, f32[144,2048]{1,0:T(8,128)S(1)}, u32[]{:S(2)}, u32[]{:S(2)}) collective-permute-start(f32[144,2048]{1,0:T(8,128)S(1)} %subtract_bitcast_fusion), channel_id=1, source_target_pairs={{0,16},{16,32},{32,48},{48,64},{64,80},{80,96},{96,112},{1,17},{17... | collective-permute-start | bytes 3538952 | tf_op jit(solution)/shard_map/ppermute | solution.py:40
  68.5 30.8 %collective-permute-start.8 = (f32[136,2048]{1,0:T(8,128)S(1)}, f32[136,2048]{1,0:T(8,128)S(1)}, u32[]{:S(2)}, u32[]{:S(2)}) collective-permute-start(f32[136,2048]{1,0:T(8,128)S(1)} %collective-permute-done.refs_1_), channel_id=1, source_target_pairs={{0,4},{1,5},{2,6},{3,7},{4,8},{5,9},{6,10},{7,11},{8,12},{9,13},{1... | collective-permute-start | bytes 3342344 | tf_op jit(solution)/shard_map/ppermute | solution.py:23
  68.6 30.8 %collective-permute-start.9 = (f32[136,2048]{1,0:T(8,128)}, f32[136,2048]{1,0:T(8,128)}, u32[]{:S(2)}, u32[]{:S(2)}) collective-permute-start(f32[136,2048]{1,0:T(8,128)} %collective-permute-done.6.refs_3_), channel_id=1, source_target_pairs={{0,12},{1,13},{2,14},{3,15},{4,0},{5,1},{6,2},{7,3},{8,4},{9,5},{1... | collective-permute-start | bytes 3342344 | tf_op jit(solution)/shard_map/ppermute | solution.py:23
  100.9 20.8 %collective-permute-start.11 = (f32[104,2048]{1,0:T(8,128)}, f32[104,2048]{1,0:T(8,128)S(1)}, u32[]{:S(2)}, u32[]{:S(2)}) collective-permute-start(f32[104,2048]{1,0:T(8,128)} %subtract_bitcast_fusion.2), channel_id=1, source_target_pairs={{0,16},{16,32},{32,48},{48,64},{64,80},{80,96},{96,112},{1,17},{17... | collective-permute-start | bytes 2555912 | tf_op jit(solution)/shard_map/ppermute | solution.py:40
  121.6 13.0 %collective-permute-start.12 = (f32[384,2048]{1,0:T(8,128)}, f32[384,2048]{1,0:T(8,128)S(1)}, u32[]{:S(2)}, u32[]{:S(2)}) collective-permute-start(f32[384,2048]{1,0:T(8,128)} %get-tuple-element.140), channel_id=1, source_target_pairs={{0,1},{1,0},{2,3},{3,2},{4,5},{5,4},{6,7},{7,6},{8,9},{9,8},{10,11... | collective-permute-start | bytes 9437192 | tf_op jit(solution)/shard_map/ppermute | solution.py:23
  121.7 28.4 %collective-permute-start.15 = (f32[136,2048]{1,0:T(8,128)}, f32[136,2048]{1,0:T(8,128)S(1)}, u32[]{:S(2)}, u32[]{:S(2)}) collective-permute-start(f32[136,2048]{1,0:T(8,128)} %get-tuple-element.151), channel_id=1, source_target_pairs={{0,4},{1,5},{2,6},{3,7},{4,8},{5,9},{6,10},{7,11},{8,12},{9,13},{1... | collective-permute-start | bytes 3342344 | tf_op jit(solution)/shard_map/ppermute | solution.py:23
  121.8 28.3 %collective-permute-start.16 = (f32[136,2048]{1,0:T(8,128)}, f32[136,2048]{1,0:T(8,128)S(1)}, u32[]{:S(2)}, u32[]{:S(2)}) collective-permute-start(f32[136,2048]{1,0:T(8,128)} %get-tuple-element.152), channel_id=1, source_target_pairs={{0,12},{1,13},{2,14},{3,15},{4,0},{5,1},{6,2},{7,3},{8,4},{9,5},{1... | collective-permute-start | bytes 3342344 | tf_op jit(solution)/shard_map/ppermute | solution.py:23
  135.1 21.2 %collective-permute-start.17 = (f32[3,384,256]{2,1,0:T(8,128)S(1)}, f32[3,384,256]{2,1,0:T(8,128)S(1)}, u32[]{:S(2)}, u32[]{:S(2)}) collective-permute-start(f32[3,384,256]{2,1,0:T(8,128)S(1)} %pad_maximum_fusion.4), channel_id=1, source_target_pairs={{0,1},{1,0},{2,3},{3,2},{4,5},{5,4},{6,7},{7,6},{8,9},{9,8},{10,11... | collective-permute-start | bytes 3538952 | tf_op jit(solution)/shard_map/ppermute | solution.py:23
  138.7 17.5 %collective-permute-start.14 = (f32[64,2048]{1,0:T(8,128)S(1)}, f32[64,2048]{1,0:T(8,128)S(1)}, u32[]{:S(2)}, u32[]{:S(2)}) collective-permute-start(f32[64,2048]{1,0:T(8,128)S(1)} %get-tuple-element.194), channel_id=1, source_target_pairs={{16,0},{32,16},{48,32},{64,48},{80,64},{96,80},{112,96},{17,1},{33... | collective-permute-start | bytes 1572872 | tf_op jit(solution)/shard_map/ppermute | solution.py:40
  156.3 25.9 %collective-permute-start.21 = (f32[136,2048]{1,0:T(8,128)S(1)}, f32[136,2048]{1,0:T(8,128)S(1)}, u32[]{:S(2)}, u32[]{:S(2)}) collective-permute-start(f32[136,2048]{1,0:T(8,128)S(1)} %get-tuple-element.172), channel_id=1, source_target_pairs={{0,12},{1,13},{2,14},{3,15},{4,0},{5,1},{6,2},{7,3},{8,4},{9,5},{1... | collective-permute-start | bytes 3342344 | tf_op jit(solution)/shard_map/ppermute | solution.py:23
  156.6 28.6 %collective-permute-start.19 = (f32[136,2048]{1,0:T(8,128)S(1)}, f32[136,2048]{1,0:T(8,128)S(1)}, u32[]{:S(2)}, u32[]{:S(2)}) collective-permute-start(f32[136,2048]{1,0:T(8,128)S(1)} %copy-done.35), channel_id=1, source_target_pairs={{0,4},{1,5},{2,6},{3,7},{4,8},{5,9},{6,10},{7,11},{8,12},{9,13},{1... | collective-permute-start | bytes 3342344 | tf_op jit(solution)/shard_map/ppermute | solution.py:23
  160.4 50.8 %collective-permute-start.13 = (f32[256,2048]{1,0:T(8,128)}, f32[256,2048]{1,0:T(8,128)}, u32[]{:S(2)}, u32[]{:S(2)}) collective-permute-start(f32[256,2048]{1,0:T(8,128)} %bitcast_subtract_fusion), channel_id=1, source_target_pairs={{16,0},{32,16},{48,32},{64,48},{80,64},{96,80},{112,96},{17,1},{33... | collective-permute-start | bytes 6291464 | tf_op jit(solution)/shard_map/ppermute | solution.py:40
  183.4 27.8 %collective-permute-start.22 = (f32[136,2048]{1,0:T(8,128)}, f32[136,2048]{1,0:T(8,128)}, u32[]{:S(2)}, u32[]{:S(2)}) collective-permute-start(f32[136,2048]{1,0:T(8,128)} %add.58), channel_id=1, source_target_pairs={{0,12},{1,13},{2,14},{3,15},{4,0},{5,1},{6,2},{7,3},{8,4},{9,5},{1... | collective-permute-start | bytes 3342344 | tf_op jit(solution)/shard_map/ppermute | solution.py:23
  186.3 26.7 %collective-permute-start.20 = (f32[136,2048]{1,0:T(8,128)}, f32[136,2048]{1,0:T(8,128)}, u32[]{:S(2)}, u32[]{:S(2)}) collective-permute-start(f32[136,2048]{1,0:T(8,128)} %add.57), channel_id=1, source_target_pairs={{0,4},{1,5},{2,6},{3,7},{4,8},{5,9},{6,10},{7,11},{8,12},{9,13},{1... | collective-permute-start | bytes 3342344 | tf_op jit(solution)/shard_map/ppermute | solution.py:23
  214.5 42.0 %collective-permute-start.24 = (f32[136,2048]{1,0:T(8,128)S(1)}, f32[136,2048]{1,0:T(8,128)}, u32[]{:S(2)}, u32[]{:S(2)}) collective-permute-start(f32[136,2048]{1,0:T(8,128)S(1)} %add.60), channel_id=1, source_target_pairs={{0,2},{1,3},{2,0},{3,1},{4,6},{5,7},{6,4},{7,5},{8,10},{9,11},{10,... | collective-permute-start | bytes 3342344 | tf_op jit(solution)/shard_map/ppermute | solution.py:23
  215.0 37.2 %collective-permute-start.23 = (f32[64,2048]{1,0:T(8,128)S(1)}, f32[64,2048]{1,0:T(8,128)S(1)}, u32[]{:S(2)}, u32[]{:S(2)}) collective-permute-start(f32[64,2048]{1,0:T(8,128)S(1)} %copy-done.16), channel_id=1, source_target_pairs={{16,0},{32,16},{48,32},{64,48},{80,64},{96,80},{112,96},{17,1},{33... | collective-permute-start | bytes 1572872 | tf_op jit(solution)/shard_map/ppermute | solution.py:40
  (37 other events, 183.5 us)

commit v4 on v3

--- a/solution.py
+++ b/solution.py
@@ -14,7 +14,7 @@
 QUAD = 4 * BLOCK
 TAU_P = 0.5
 TILES = 2
-EARLY_TILES = 4
+EARLY_TILES = 2
 WIDE = 512
 SMALL = pl.CostEstimate(flops=1024, bytes_accessed=1024, transcendentals=0)
 
@@ -350,7 +350,7 @@
     hold = lax.optimization_barrier
     parts = [slice(0, 64), slice(64, 320), slice(320, 384)]
 
-    cuts = [slice(0, 136), slice(136, 280), slice(280, 384)]
+    cuts = [slice(0, 112), slice(112, 264), slice(264, 384)]
     bias_rows = jnp.pad(offsets, ((0, 7), (0, D - BLOCK)))
     w = jnp.concatenate([w, bias_rows], axis=0)
     w_x = x_swap(w)

time: 261 us -> 259 us (level)
    unnamed x74 -> x72, local copies, waits for them, and re-layouts: 16.6 us -> 15.9 us
  transfers between devices with their start and end apart: 25 -> 25, of which waited for: 10 -> 11; matrix products, arithmetic and copies ran while one was open for 11% -> 11% of each run, Pallas kernels for 31% -> 31%
where the time goes in v4:
time: 259 us
  waiting for transfers between devices  89.3 us (34%)
  Pallas kernels  79.9 us (31%)
  starting transfers between devices  38.3 us (15%)
  other arithmetic  33.8 us (13%)
  local copies, waits for them, and re-layouts  16.2 us (6%)
    pallas_call x4, Pallas kernels, in_tiles(): pl.pallas_call(kernel, grid=(tiles,), out_shape=tuple(out_shape), in_spec...  61.4 us
    ppermute x6, waiting for transfers between devices, depth_shift(): lax.ppermute(v, 'depth', [(i, i + k) for i in range(n) if 0 <= i + k < n])  49.6 us
    ppermute x19, waiting for transfers between devices, dp_move(): return lax.ppermute(v, 'dp', [(i, step(i)) for i in range(16)])  39.7 us
    ppermute x19, starting transfers between devices, dp_move(): return lax.ppermute(v, 'dp', [(i, step(i)) for i in range(16)])  19.6 us
    ppermute x6, starting transfers between devices, depth_shift(): lax.ppermute(v, 'depth', [(i, i + k) for i in range(n) if 0 <= i + k < n])  18.7 us
    unnamed x72, local copies, waits for them, and re-layouts  15.9 us
    pallas_call x3, Pallas kernels, last_step(): pl.pallas_call(last_kernel, out_shape=(out, out), grid_spec=pltpu.Prefetc...  13.6 us
    sub x3, other arithmetic, body(): ahead = [u[t] - q[t] for t in cuts]  6.08 us
  transfers between devices with their start and end apart: 25, of which 11 were waited for; matrix products, arithmetic and copies ran while one was open for 11% of the time, Pallas kernels for 31%

profile of v4, /device:TPU:0, one launch (start us, length us, event | category | flops | bytes accessed | tf_op | source)
XLA Modules:
  0.0 258.6 jit_solution(7280477261357327055)
XLA Ops:
  7.6 5.0 %parity.1 = (f32[4,384,256]{2,1,0:T(8,128)}, f32[4,384,256]{2,1,0:T(8,128)}) custom-call(s32[4]{0:T(128)} %pad_add_fusion.s_ref, f32[384,2048]{1,0:T(8,128)} %bitcast.51), custom_call_target="tpu_custom_call" | custom-call | flops 1024 | bytes 1024 | tf_op jit(solution)/shard_map/parity/pallas_call | solution.py:61
  12.6 2.6 subtract_bitcast_fusion.1
  19.4 6.0 %fusion = (bf16[768,2048]{1,0:T(8,128)(2,1)}, bf16[768,2048]{1,0:T(8,128)(2,1)}) fusion(f32[384,2048]{1,0:T(8,128)} %collective-permute-done.3, f32[384,2048]{1,0:T(8,128)S(1)} %bitcast.59), kind=kLoop, calls=%fused_computation.2 | loop fusion | flops 7864320 | bytes 12582912 | tf_op jit(solution)/shard_map/convert_element_type | solution.py:364
  25.3 3.8 %collective-permute-done.refs_1_ = f32[136,2048]{1,0:T(8,128)S(1)} collective-permute-done((f32[136,2048]{1,0:T(8,128)S(1)}, f32[136,2048]{1,0:T(8,128)S(1)}, u32[]{:S(2)}, u32[]{:S(2)}) %collective-permute-start) | collective-permute-done | bytes 1114144 | tf_op jit(solution)/shard_map/ppermute | solution.py:23
  29.1 2.7 %collective-permute-done.1.refs_0_ = f32[136,2048]{1,0:T(8,128)} collective-permute-done((f32[136,2048]{1,0:T(8,128)S(1)}, f32[136,2048]{1,0:T(8,128)}, u32[]{:S(2)}, u32[]{:S(2)}) %collective-permute-start.1) | collective-permute-done | bytes 1114144 | tf_op jit(solution)/shard_map/ppermute | solution.py:23
  35.1 4.7 %collective-permute-start.7 = (f32[112,2048]{1,0:T(8,128)S(1)}, f32[112,2048]{1,0:T(8,128)S(1)}, u32[]{:S(2)}, u32[]{:S(2)}) collective-permute-start(f32[112,2048]{1,0:T(8,128)S(1)} %subtract_bitcast_fusion.2), channel_id=1, source_target_pairs={{0,16},{16,32},{32,48},{48,64},{64,80},{80,96},{96,112},{1,17},{17... | collective-permute-start | bytes 2752520 | tf_op jit(solution)/shard_map/ppermute | solution.py:40
  41.7 14.1 %layer_step.2 = (f32[768,2048]{1,0:T(8,128)}, f32[768,256]{1,0:T(8,128)S(1)}, f32[136,2048]{1,0:T(8,128)S(1)}, f32[136,2048]{1,0:T(8,128)S(1)}) custom-call(bf16[768,2048]{1,0:T(8,128)(2,1)} %get-tuple-element.113.ph_ref, bf16[768,2048]{1,0:T(8,128)(2,1)} %get-tuple-element.114.pl_ref, f32[136,2048]{1,0:T(8,128)S(1)} %select_maximum_fusion.refs_0_, ...), custom_call_target="tpu_custom_call" | custom-call | flops 1024 | bytes 1024 | tf_op jit(solution)/shard_map/layer_step/pallas_call | solution.py:247
  59.2 5.2 %collective-permute-start.10 = (f32[152,2048]{1,0:T(8,128)S(1)}, f32[152,2048]{1,0:T(8,128)S(1)}, u32[]{:S(2)}, u32[]{:S(2)}) collective-permute-start(f32[152,2048]{1,0:T(8,128)S(1)} %subtract_bitcast_fusion), channel_id=1, source_target_pairs={{0,16},{16,32},{32,48},{48,64},{64,80},{80,96},{96,112},{1,17},{17... | collective-permute-start | bytes 3735560 | tf_op jit(solution)/shard_map/ppermute | solution.py:40
  64.8 2.8 %collective-permute-start.9 = (f32[136,2048]{1,0:T(8,128)}, f32[136,2048]{1,0:T(8,128)}, u32[]{:S(2)}, u32[]{:S(2)}) collective-permute-start(f32[136,2048]{1,0:T(8,128)} %collective-permute-done.6.refs_3_), channel_id=1, source_target_pairs={{0,12},{1,13},{2,14},{3,15},{4,0},{5,1},{6,2},{7,3},{8,4},{9,5},{1... | collective-permute-start | bytes 3342344 | tf_op jit(solution)/shard_map/ppermute | solution.py:23
  67.6 27.6 %layer_step.3 = (f32[768,2048]{1,0:T(8,128)}, f32[768,512]{1,0:T(8,128)}, f32[136,2048]{1,0:T(8,128)}, f32[136,2048]{1,0:T(8,128)}, f32[136,2048]{1,0:T(8,128)}, /*index=5*/f32[136,2048]{1,0:T(8,128)}) custom-call(bf16[768,2048]{1,0:T(8,128)(2,1)} %get-tuple-element.113.ph_ref, ...), custom_call_target="tpu_custom_call", output_to_operand_aliasing={{0}: (10, {})} | custom-call | flops 1024 | bytes 1024 | tf_op jit(solution)/shard_map/layer_step/pallas_call | solution.py:247
  96.7 4.9 %collective-permute-start.11 = (f32[120,2048]{1,0:T(8,128)}, f32[120,2048]{1,0:T(8,128)S(1)}, u32[]{:S(2)}, u32[]{:S(2)}) collective-permute-start(f32[120,2048]{1,0:T(8,128)} %subtract_bitcast_fusion.1), channel_id=1, source_target_pairs={{0,16},{16,32},{32,48},{48,64},{64,80},{80,96},{96,112},{1,17},{17... | collective-permute-start | bytes 2949128 | tf_op jit(solution)/shard_map/ppermute | solution.py:40
  101.7 14.6 %early_step.1 = (f32[384,2048]{1,0:T(8,128)}, f32[384,2048]{1,0:T(8,128)}, f32[768,256]{1,0:T(8,128)}, bf16[768,256]{1,0:T(8,128)(2,1)}, bf16[768,256]{1,0:T(8,128)(2,1)}, /*index=5*/f32[1,256]{1,0:T(1,128)}) custom-call(bf16[768,2048]{1,0:T(8,128)(2,1)} %get-tuple-element.113.ph_ref, bf16[768,2048]{1,0:T(8,128)(2,1)} %get-tuple-element.114.pl_ref, ...), custom_call_target="tpu_custom_call" | custom-call | flops 1024 | bytes 1024 | tf_op jit(solution)/shard_map/early_step/pallas_call | solution.py:247
  116.3 3.9 %collective-permute-done.11 = f32[120,2048]{1,0:T(8,128)S(1)} collective-permute-done((f32[120,2048]{1,0:T(8,128)}, f32[120,2048]{1,0:T(8,128)S(1)}, u32[]{:S(2)}, u32[]{:S(2)}) %collective-permute-start.11) | collective-permute-done | bytes 983072 | tf_op jit(solution)/shard_map/ppermute | solution.py:40
  120.2 3.2 %collective-permute-start.16 = (f32[136,2048]{1,0:T(8,128)}, f32[136,2048]{1,0:T(8,128)S(1)}, u32[]{:S(2)}, u32[]{:S(2)}) collective-permute-start(f32[136,2048]{1,0:T(8,128)} %get-tuple-element.152), channel_id=1, source_target_pairs={{0,12},{1,13},{2,14},{3,15},{4,0},{5,1},{6,2},{7,3},{8,4},{9,5},{1... | collective-permute-start | bytes 3342344 | tf_op jit(solution)/shard_map/ppermute | solution.py:23
  127.9 5.0 %late_step.1 = (f32[136,2048]{1,0:T(8,128)S(1)}, f32[136,2048]{1,0:T(8,128)S(1)}) custom-call(bf16[768,2048]{1,0:T(8,128)(2,1)S(1)} %copy-done.1, bf16[768,2048]{1,0:T(8,128)(2,1)S(1)} %copy-done, bf16[768,256]{1,0:T(8,128)(2,1)S(1)} %copy-done.6, bf16[768,256]{1,0:T(8,128)(2,1)S(1)} %copy-done.7, f32[1,256]{1,0:T(1,128)S(1)} %copy-done.8), custom_call_target="tpu_custom_call" | custom-call | flops 1024 | bytes 1024 | tf_op jit(solution)/shard_map/late_step/pallas_call | solution.py:247
  138.5 10.1 %collective-permute-done.15 = f32[136,2048]{1,0:T(8,128)S(1)} collective-permute-done((f32[136,2048]{1,0:T(8,128)}, f32[136,2048]{1,0:T(8,128)S(1)}, u32[]{:S(2)}, u32[]{:S(2)}) %collective-permute-start.15) | collective-permute-done | bytes 1114144 | tf_op jit(solution)/shard_map/ppermute | solution.py:23
  150.5 4.4 %collective-permute-done.14.r_ref = f32[64,2048]{1,0:T(8,128)S(1)} collective-permute-done((f32[64,2048]{1,0:T(8,128)S(1)}, f32[64,2048]{1,0:T(8,128)S(1)}, u32[]{:S(2)}, u32[]{:S(2)}) %collective-permute-start.14) | collective-permute-done | bytes 524320 | tf_op jit(solution)/shard_map/ppermute | solution.py:40
  160.4 20.4 %collective-permute-done.21 = f32[136,2048]{1,0:T(8,128)S(1)} collective-permute-done((f32[136,2048]{1,0:T(8,128)S(1)}, f32[136,2048]{1,0:T(8,128)S(1)}, u32[]{:S(2)}, u32[]{:S(2)}) %collective-permute-start.21) | collective-permute-done | bytes 1114144 | tf_op jit(solution)/shard_map/ppermute | solution.py:23
  185.2 4.5 %fusion.1 = f32[384,2048]{1,0:T(8,128)} fusion(f32[64,2048]{1,0:T(8,128)} %get-tuple-element.182, f32[256,2048]{1,0:T(8,128)} %bitcast_subtract_fusion, f32[64,2048]{1,0:T(8,128)} %copy-done.16, f32[120,2048]{1,0:T(8,128)} %copy-done.28, f32[152,2048]{1,0:T(8,128)} %copy-done.19, f32[112,2048]{1,0:T(8,128)} %copy-done.29, pred[]{:T(512)S(6)} %eq.10, ...), kind=kLoop, calls=%fused_computation.5 | loop fusion | flops 5505024 | bytes 12582913 | tf_op jit(solution)/shard_map/jit(_where)/select_n | solution.py:412
  191.0 3.5 %last_step.3 = (f32[384,2048]{1,0:T(8,128)}, f32[384,2048]{1,0:T(8,128)}) custom-call(s32[4]{0:T(128)} %pad_add_fusion.s_ref, f32[4,384,256]{2,1,0:T(8,128)} %pad_maximum_fusion.1.mine_ref, f32[4,384,256]{2,1,0:T(8,128)} %copy-done.12, f32[64,2048]{1,0:T(8,128)} %copy-done.31, f32[384,2048]{1,0:T(8,128)} %bitcast.52, f32[384,2048]{1,0:T(8,128)} %bitcast.55), custom_call_target="tpu_custom_call" | custom-call | flops 1024 | bytes 1024 | tf_op jit(solution)/shard_map/last_step/pallas_call | solution.py:104
  196.5 13.2 %collective-permute-done.13.r_ref = f32[256,2048]{1,0:T(8,128)} collective-permute-done((f32[256,2048]{1,0:T(8,128)}, f32[256,2048]{1,0:T(8,128)}, u32[]{:S(2)}, u32[]{:S(2)}) %collective-permute-start.13) | collective-permute-done | bytes 2097184 | tf_op jit(solution)/shard_map/ppermute | solution.py:40
  214.9 6.7 %last_step.4 = (f32[384,2048]{1,0:T(8,128)}, f32[384,2048]{1,0:T(8,128)}) custom-call(s32[4]{0:T(128)} %pad_add_fusion.s_ref, f32[4,384,256]{2,1,0:T(8,128)} %pad_maximum_fusion.1.mine_ref, f32[4,384,256]{2,1,0:T(8,128)} %copy-done.12, f32[256,2048]{1,0:T(8,128)} %collective-permute-done.13.r_ref, ...), custom_call_target="tpu_custom_call", output_to_operand_aliasing={{0}: (6, {}), {1}: (7, {})} | custom-call | flops 1024 | bytes 1024 | tf_op jit(solution)/shard_map/last_step/pallas_call | solution.py:104
  223.3 27.6 %collective-permute-done.23.r_ref = f32[64,2048]{1,0:T(8,128)S(1)} collective-permute-done((f32[64,2048]{1,0:T(8,128)S(1)}, f32[64,2048]{1,0:T(8,128)S(1)}, u32[]{:S(2)}, u32[]{:S(2)}) %collective-permute-start.23) | collective-permute-done | bytes 524320 | tf_op jit(solution)/shard_map/ppermute | solution.py:40
  251.6 3.4 %last_step.5 = (f32[384,2048]{1,0:T(8,128)}, f32[384,2048]{1,0:T(8,128)}) custom-call(s32[4]{0:T(128)} %pad_add_fusion.s_ref, f32[4,384,256]{2,1,0:T(8,128)} %pad_maximum_fusion.1.mine_ref, f32[4,384,256]{2,1,0:T(8,128)} %copy-done.12, f32[64,2048]{1,0:T(8,128)} %copy-done.32, f32[384,2048]{1,0:T(8,128)} %bitcast.54, ...), custom_call_target="tpu_custom_call", output_to_operand_aliasing={{0}: (6, {}), {1}: (7, {})} | custom-call | flops 1024 | bytes 1024 | tf_op jit(solution)/shard_map/last_step/pallas_call | solution.py:104
  (134 shorter events, 57.7 us)
Async XLA Ops:
  0.6 18.1 %collective-permute-start.3 = (f32[384,2048]{1,0:T(8,128)}, f32[384,2048]{1,0:T(8,128)}, u32[]{:S(2)}, u32[]{:S(2)}) collective-permute-start(f32[384,2048]{1,0:T(8,128)} %bitcast.58), channel_id=1, source_target_pairs={{0,1},{1,0},{2,3},{3,2},{4,5},{5,4},{6,7},{7,6},{8,9},{9,8},{10,11... | collective-permute-start | bytes 9437192 | tf_op jit(solution)/shard_map/ppermute | solution.py:23
  2.1 27.0 %collective-permute-start = (f32[136,2048]{1,0:T(8,128)S(1)}, f32[136,2048]{1,0:T(8,128)S(1)}, u32[]{:S(2)}, u32[]{:S(2)}) collective-permute-start(f32[136,2048]{1,0:T(8,128)S(1)} %select_maximum_fusion.refs_0_), channel_id=1, source_target_pairs={{0,2},{1,3},{2,0},{3,1},{4,6},{5,7},{6,4},{7,5},{8,10},{9,11},{10,... | collective-permute-start | bytes 3342344 | tf_op jit(solution)/shard_map/ppermute | solution.py:23
  3.7 28.1 %collective-permute-start.1 = (f32[136,2048]{1,0:T(8,128)S(1)}, f32[136,2048]{1,0:T(8,128)}, u32[]{:S(2)}, u32[]{:S(2)}) collective-permute-start(f32[136,2048]{1,0:T(8,128)S(1)} %select_maximum_fusion.refs_0_), channel_id=1, source_target_pairs={{0,4},{1,5},{2,6},{3,7},{4,8},{5,9},{6,10},{7,11},{8,12},{9,13},{1... | collective-permute-start | bytes 3342344 | tf_op jit(solution)/shard_map/ppermute | solution.py:23
  5.3 26.5 %collective-permute-start.2 = (f32[136,2048]{1,0:T(8,128)S(1)}, f32[136,2048]{1,0:T(8,128)}, u32[]{:S(2)}, u32[]{:S(2)}) collective-permute-start(f32[136,2048]{1,0:T(8,128)S(1)} %select_maximum_fusion.refs_0_), channel_id=1, source_target_pairs={{0,12},{1,13},{2,14},{3,15},{4,0},{5,1},{6,2},{7,3},{8,4},{9,5},{1... | collective-permute-start | bytes 3342344 | tf_op jit(solution)/shard_map/ppermute | solution.py:23
  12.6 19.2 %collective-permute-start.4 = (f32[4,384,256]{2,1,0:T(8,128)}, f32[4,384,256]{2,1,0:T(8,128)S(1)}, u32[]{:S(2)}, u32[]{:S(2)}) collective-permute-start(f32[4,384,256]{2,1,0:T(8,128)} %get-tuple-element.101), channel_id=1, source_target_pairs={{0,1},{1,0},{2,3},{3,2},{4,5},{5,4},{6,7},{7,6},{8,9},{9,8},{10,11... | collective-permute-start | bytes 4718600 | tf_op jit(solution)/shard_map/ppermute | solution.py:23
  31.8 27.3 %collective-permute-start.5 = (f32[136,2048]{1,0:T(8,128)}, f32[136,2048]{1,0:T(8,128)S(1)}, u32[]{:S(2)}, u32[]{:S(2)}) collective-permute-start(f32[136,2048]{1,0:T(8,128)} %collective-permute-done.1.refs_0_), channel_id=1, source_target_pairs={{0,4},{1,5},{2,6},{3,7},{4,8},{5,9},{6,10},{7,11},{8,12},{9,13},{1... | collective-permute-start | bytes 3342344 | tf_op jit(solution)/shard_map/ppermute | solution.py:23
  33.4 25.8 %collective-permute-start.6 = (f32[136,2048]{1,0:T(8,128)S(1)}, f32[136,2048]{1,0:T(8,128)}, u32[]{:S(2)}, u32[]{:S(2)}) collective-permute-start(f32[136,2048]{1,0:T(8,128)S(1)} %collective-permute-done.refs_1_), channel_id=1, source_target_pairs={{0,12},{1,13},{2,14},{3,15},{4,0},{5,1},{6,2},{7,3},{8,4},{9,5},{1... | collective-permute-start | bytes 3342344 | tf_op jit(solution)/shard_map/ppermute | solution.py:23
  35.1 23.3 %collective-permute-start.7 = (f32[112,2048]{1,0:T(8,128)S(1)}, f32[112,2048]{1,0:T(8,128)S(1)}, u32[]{:S(2)}, u32[]{:S(2)}) collective-permute-start(f32[112,2048]{1,0:T(8,128)S(1)} %subtract_bitcast_fusion.2), channel_id=1, source_target_pairs={{0,16},{16,32},{32,48},{48,64},{64,80},{80,96},{96,112},{1,17},{17... | collective-permute-start | bytes 2752520 | tf_op jit(solution)/shard_map/ppermute | solution.py:40
  59.2 36.1 %collective-permute-start.10 = (f32[152,2048]{1,0:T(8,128)S(1)}, f32[152,2048]{1,0:T(8,128)S(1)}, u32[]{:S(2)}, u32[]{:S(2)}) collective-permute-start(f32[152,2048]{1,0:T(8,128)S(1)} %subtract_bitcast_fusion), channel_id=1, source_target_pairs={{0,16},{16,32},{32,48},{48,64},{64,80},{80,96},{96,112},{1,17},{17... | collective-permute-start | bytes 3735560 | tf_op jit(solution)/shard_map/ppermute | solution.py:40
  64.3 30.9 %collective-permute-start.8 = (f32[136,2048]{1,0:T(8,128)S(1)}, f32[136,2048]{1,0:T(8,128)S(1)}, u32[]{:S(2)}, u32[]{:S(2)}) collective-permute-start(f32[136,2048]{1,0:T(8,128)S(1)} %collective-permute-done.refs_1_), channel_id=1, source_target_pairs={{0,4},{1,5},{2,6},{3,7},{4,8},{5,9},{6,10},{7,11},{8,12},{9,13},{1... | collective-permute-start | bytes 3342344 | tf_op jit(solution)/shard_map/ppermute | solution.py:23
  64.8 30.4 %collective-permute-start.9 = (f32[136,2048]{1,0:T(8,128)}, f32[136,2048]{1,0:T(8,128)}, u32[]{:S(2)}, u32[]{:S(2)}) collective-permute-start(f32[136,2048]{1,0:T(8,128)} %collective-permute-done.6.refs_3_), channel_id=1, source_target_pairs={{0,12},{1,13},{2,14},{3,15},{4,0},{5,1},{6,2},{7,3},{8,4},{9,5},{1... | collective-permute-start | bytes 3342344 | tf_op jit(solution)/shard_map/ppermute | solution.py:23
  96.7 23.5 %collective-permute-start.11 = (f32[120,2048]{1,0:T(8,128)}, f32[120,2048]{1,0:T(8,128)S(1)}, u32[]{:S(2)}, u32[]{:S(2)}) collective-permute-start(f32[120,2048]{1,0:T(8,128)} %subtract_bitcast_fusion.1), channel_id=1, source_target_pairs={{0,16},{16,32},{32,48},{48,64},{64,80},{80,96},{96,112},{1,17},{17... | collective-permute-start | bytes 2949128 | tf_op jit(solution)/shard_map/ppermute | solution.py:40
  120.2 12.8 %collective-permute-start.12 = (f32[384,2048]{1,0:T(8,128)}, f32[384,2048]{1,0:T(8,128)S(1)}, u32[]{:S(2)}, u32[]{:S(2)}) collective-permute-start(f32[384,2048]{1,0:T(8,128)} %get-tuple-element.140), channel_id=1, source_target_pairs={{0,1},{1,0},{2,3},{3,2},{4,5},{5,4},{6,7},{7,6},{8,9},{9,8},{10,11... | collective-permute-start | bytes 9437192 | tf_op jit(solution)/shard_map/ppermute | solution.py:23
  120.2 28.4 %collective-permute-start.15 = (f32[136,2048]{1,0:T(8,128)}, f32[136,2048]{1,0:T(8,128)S(1)}, u32[]{:S(2)}, u32[]{:S(2)}) collective-permute-start(f32[136,2048]{1,0:T(8,128)} %get-tuple-element.151), channel_id=1, source_target_pairs={{0,4},{1,5},{2,6},{3,7},{4,8},{5,9},{6,10},{7,11},{8,12},{9,13},{1... | collective-permute-start | bytes 3342344 | tf_op jit(solution)/shard_map/ppermute | solution.py:23
  120.2 28.4 %collective-permute-start.16 = (f32[136,2048]{1,0:T(8,128)}, f32[136,2048]{1,0:T(8,128)S(1)}, u32[]{:S(2)}, u32[]{:S(2)}) collective-permute-start(f32[136,2048]{1,0:T(8,128)} %get-tuple-element.152), channel_id=1, source_target_pairs={{0,12},{1,13},{2,14},{3,15},{4,0},{5,1},{6,2},{7,3},{8,4},{9,5},{1... | collective-permute-start | bytes 3342344 | tf_op jit(solution)/shard_map/ppermute | solution.py:23
  133.4 21.5 %collective-permute-start.17 = (f32[3,384,256]{2,1,0:T(8,128)S(1)}, f32[3,384,256]{2,1,0:T(8,128)S(1)}, u32[]{:S(2)}, u32[]{:S(2)}) collective-permute-start(f32[3,384,256]{2,1,0:T(8,128)S(1)} %pad_maximum_fusion.4), channel_id=1, source_target_pairs={{0,1},{1,0},{2,3},{3,2},{4,5},{5,4},{6,7},{7,6},{8,9},{9,8},{10,11... | collective-permute-start | bytes 3538952 | tf_op jit(solution)/shard_map/ppermute | solution.py:23
  137.1 17.8 %collective-permute-start.14 = (f32[64,2048]{1,0:T(8,128)S(1)}, f32[64,2048]{1,0:T(8,128)S(1)}, u32[]{:S(2)}, u32[]{:S(2)}) collective-permute-start(f32[64,2048]{1,0:T(8,128)S(1)} %get-tuple-element.194), channel_id=1, source_target_pairs={{16,0},{32,16},{48,32},{64,48},{80,64},{96,80},{112,96},{17,1},{33... | collective-permute-start | bytes 1572872 | tf_op jit(solution)/shard_map/ppermute | solution.py:40
  154.9 25.9 %collective-permute-start.21 = (f32[136,2048]{1,0:T(8,128)S(1)}, f32[136,2048]{1,0:T(8,128)S(1)}, u32[]{:S(2)}, u32[]{:S(2)}) collective-permute-start(f32[136,2048]{1,0:T(8,128)S(1)} %get-tuple-element.172), channel_id=1, source_target_pairs={{0,12},{1,13},{2,14},{3,15},{4,0},{5,1},{6,2},{7,3},{8,4},{9,5},{1... | collective-permute-start | bytes 3342344 | tf_op jit(solution)/shard_map/ppermute | solution.py:23
  155.2 28.6 %collective-permute-start.19 = (f32[136,2048]{1,0:T(8,128)S(1)}, f32[136,2048]{1,0:T(8,128)S(1)}, u32[]{:S(2)}, u32[]{:S(2)}) collective-permute-start(f32[136,2048]{1,0:T(8,128)S(1)} %copy-done.34), channel_id=1, source_target_pairs={{0,4},{1,5},{2,6},{3,7},{4,8},{5,9},{6,10},{7,11},{8,12},{9,13},{1... | collective-permute-start | bytes 3342344 | tf_op jit(solution)/shard_map/ppermute | solution.py:23
  159.0 50.8 %collective-permute-start.13 = (f32[256,2048]{1,0:T(8,128)}, f32[256,2048]{1,0:T(8,128)}, u32[]{:S(2)}, u32[]{:S(2)}) collective-permute-start(f32[256,2048]{1,0:T(8,128)} %bitcast_subtract_fusion), channel_id=1, source_target_pairs={{16,0},{32,16},{48,32},{64,48},{80,64},{96,80},{112,96},{17,1},{33... | collective-permute-start | bytes 6291464 | tf_op jit(solution)/shard_map/ppermute | solution.py:40
  182.0 27.8 %collective-permute-start.22 = (f32[136,2048]{1,0:T(8,128)}, f32[136,2048]{1,0:T(8,128)}, u32[]{:S(2)}, u32[]{:S(2)}) collective-permute-start(f32[136,2048]{1,0:T(8,128)} %add.58), channel_id=1, source_target_pairs={{0,12},{1,13},{2,14},{3,15},{4,0},{5,1},{6,2},{7,3},{8,4},{9,5},{1... | collective-permute-start | bytes 3342344 | tf_op jit(solution)/shard_map/ppermute | solution.py:23
  184.9 26.7 %collective-permute-start.20 = (f32[136,2048]{1,0:T(8,128)}, f32[136,2048]{1,0:T(8,128)}, u32[]{:S(2)}, u32[]{:S(2)}) collective-permute-start(f32[136,2048]{1,0:T(8,128)} %add.57), channel_id=1, source_target_pairs={{0,4},{1,5},{2,6},{3,7},{4,8},{5,9},{6,10},{7,11},{8,12},{9,13},{1... | collective-permute-start | bytes 3342344 | tf_op jit(solution)/shard_map/ppermute | solution.py:23
  213.1 42.0 %collective-permute-start.24 = (f32[136,2048]{1,0:T(8,128)S(1)}, f32[136,2048]{1,0:T(8,128)}, u32[]{:S(2)}, u32[]{:S(2)}) collective-permute-start(f32[136,2048]{1,0:T(8,128)S(1)} %add.60), channel_id=1, source_target_pairs={{0,2},{1,3},{2,0},{3,1},{4,6},{5,7},{6,4},{7,5},{8,10},{9,11},{10,... | collective-permute-start | bytes 3342344 | tf_op jit(solution)/shard_map/ppermute | solution.py:23
  213.6 37.2 %collective-permute-start.23 = (f32[64,2048]{1,0:T(8,128)S(1)}, f32[64,2048]{1,0:T(8,128)S(1)}, u32[]{:S(2)}, u32[]{:S(2)}) collective-permute-start(f32[64,2048]{1,0:T(8,128)S(1)} %copy-done.15), channel_id=1, source_target_pairs={{16,0},{32,16},{48,32},{64,48},{80,64},{96,80},{112,96},{17,1},{33... | collective-permute-start | bytes 1572872 | tf_op jit(solution)/shard_map/ppermute | solution.py:40
  (36 other events, 180.8 us)
